TPU v7x, 256 devices: a whole 4x4x8 slice. The times are simulated.
256 devices in a mesh: space: 32 (over x, z), chan: 8 (over y, core).
Axes of the slice: x: 4, y: 4, z: 8, core: 2. Of those that a mesh axis runs over, the one named last changes fastest.
Arguments:
- hidden: bfloat16 [96, 147456], P('space', 'chan'), may hold values from -3 to 3
- conditioning: bfloat16 [2, 96, 36864], P(None, 'space', 'chan'), may hold values from -6 to 6
- gate_weight: bfloat16 [1920, 27648], P('space', 'chan'), may hold values from -0.046875 to 0.046875
- gate_bias: float32 [2, 1536], P(None, 'chan'), may hold values from -4 to 4
- cand_weight: bfloat16 [960, 27648], P('space', 'chan'), may hold values from -0.046875 to 0.046875
- cand_bias: float32 [1536], P('chan'), may hold values from -4 to 4
Outputs:
- states: bfloat16 [2, 96, 147456], P(None, 'space', 'chan')
All inputs are finite; a program needn't handle non-finite values.
Results may differ from a plain program's by a relative error of at most 0.0026.
Values may be sent and summed in bfloat16 or wider, within the bound.
A program may use at most 192 MiB of HBM per device.

v0:
```python
import jax
import jax.numpy as jnp
from jax import lax
from jax.sharding import PartitionSpec as P

W = 96


def with_halo(block, sides, width):
    for axis, dim in sides:
        count = lax.axis_size(axis)
        forward = [(i, i + 1) for i in range(count - 1)]
        backward = [(target, source) for source, target in forward]
        low = lax.ppermute(
            lax.slice_in_dim(block, block.shape[dim] - width, None, axis=dim), axis, forward
        )
        high = lax.ppermute(lax.slice_in_dim(block, 0, width, axis=dim), axis, backward)
        block = jnp.concatenate([low, block, high], axis=dim)
    return block


def convolve(padded, kernel):
    row_count = padded.shape[0] - 2
    col_count = padded.shape[1] - 2
    channels = padded.shape[2]
    running = jnp.zeros((row_count * col_count, kernel.shape[3]), jnp.float32)
    for tap_row in range(3):
        for tap_col in range(3):
            window = padded[
                tap_row : tap_row + row_count, tap_col : tap_col + col_count, :
            ].reshape(row_count * col_count, channels)
            running = running + jnp.dot(
                window, kernel[tap_row, tap_col], preferred_element_type=jnp.float32
            )
    return running


def gate_taps(raw, own):
    count = raw.shape[0]
    return raw.reshape(count, own, 2, 3, 3).transpose(3, 4, 0, 2, 1).reshape(3, 3, count, 2 * own)


def cand_taps(raw, own):
    count = raw.shape[0]
    return raw.reshape(count, own, 2, 3, 3).transpose(3, 4, 0, 2, 1).reshape(3, 3, 2 * count, own)


def pad_sides(field):
    return jnp.pad(field, ((0, 0), (1, 1), (0, 0)))


def gather_inputs(cond_now, state_now):
    cond_full, state_full = (
        lax.all_gather(cond_now, "chan", axis=2, tiled=True),
        lax.all_gather(state_now, "chan", axis=2, tiled=True),
    )
    joined = jnp.concatenate([cond_full, state_full], axis=2)
    rimmed = with_halo(joined, (("space", 0),), 1)
    return pad_sides(rimmed)


def gather_gated(gated):
    gated_full = lax.all_gather(gated, "chan", axis=2, tiled=True)
    rimmed = with_halo(gated_full, (("space", 0),), 1)
    return pad_sides(rimmed)


def local(hidden, conditioning, gate_weight, gate_bias, cand_weight, cand_bias):
    moments = conditioning.shape[0]
    col_count = W
    row_count = hidden.shape[0]
    own = hidden.shape[1] // col_count
    cond_own = conditioning.shape[2] // col_count
    cond_grid = conditioning.reshape(moments, row_count, cond_own, col_count).transpose(0, 1, 3, 2)
    cond_total = cond_own * lax.axis_size("chan")
    gate_shift = gate_bias.reshape(2 * own)
    gate_full, cand_full = (
        lax.all_gather(gate_weight, "space", axis=0, tiled=True),
        lax.all_gather(cand_weight, "space", axis=0, tiled=True),
    )
    gate_kernel = gate_taps(gate_full, own)
    cand_kernel = cand_taps(cand_full, own)
    state = hidden.reshape(row_count, own, col_count).transpose(0, 2, 1)
    frames = []
    for moment in range(moments):
        padded = gather_inputs(cond_grid[moment], state)
        gate_sum = convolve(padded, gate_kernel)
        preact = gate_sum + gate_shift
        update = jax.nn.sigmoid(preact[:, :own])
        reset = jax.nn.sigmoid(preact[:, own:])
        previous = state.astype(jnp.float32).reshape(row_count * col_count, own)
        gated = (reset * previous).astype(jnp.bfloat16).reshape(row_count, col_count, own)
        gated_padded = gather_gated(gated)
        cand_input = jnp.concatenate([padded[:, :, :cond_total], gated_padded], axis=2)
        cand_sum = convolve(cand_input, cand_kernel)
        candidate = jnp.tanh(cand_sum + cand_bias)
        state = (
            ((1.0 - update) * previous + update * candidate)
            .astype(jnp.bfloat16)
            .reshape(row_count, col_count, own)
        )
        frames.append(state.transpose(0, 2, 1).reshape(row_count, own * col_count))
    return jnp.stack(frames)


def solution(mesh):
    placed = (
        P("space", "chan"),
        P(None, "space", "chan"),
        P("space", "chan"),
        P(None, "chan"),
        P("space", "chan"),
        P("chan"),
    )
    return jax.shard_map(
        local, mesh=mesh, in_specs=placed, out_specs=P(None, "space", "chan"), check_vma=False
    )
```

profile of v0, /device:TPU:31, one launch (start us, length us, event | category | flops | bytes accessed | tf_op | source)
XLA Modules:
  0.0 578.5 jit_solution(10733711650661361821)
XLA Ops:
  9.2 15.3 %all_gather.25 = bf16[3,96,1536]{1,0,2:T(4,128)(2,1)S(1)} all-gather(bf16[3,96,192]{1,0,2:T(4,128)(2,1)S(1)} %copy.36), channel_id=1, replica_groups=mesh['space'=32,'chan'=8] {'chan'}, dimensions={2}, use_global_device_ids=true | all-gather | bytes 995328 | tf_op jit(solution)/shard_map/all_gather | solution.py:55
  26.1 12.8 %all-gather = bf16[1,3,96,384]{2,3,1,0:T(8,128)(2,1)S(1)} all-gather(bf16[1,3,96,48]{2,3,1,0:T(8,128)(2,1)S(1)} %get-tuple-element.52), channel_id=2, replica_groups=mesh['space'=32,'chan'=8] {'chan'}, dimensions={3}, use_global_device_ids=true | all-gather | bytes 248832 | tf_op jit(solution)/shard_map/all_gather | solution.py:54
  39.2 7.7 %collective-permute-start.1 = (bf16[1,96,1920]{2,1,0:T(8,128)(2,1)S(1)}, bf16[1,96,1920]{2,1,0:T(8,128)(2,1)S(1)}, u32[]{:S(2)}, u32[]{:S(2)}) collective-permute-start(bf16[1,96,1920]{2,1,0:T(8,128)(2,1)S(1)} %get-tuple-element.44), channel_id=1, source_target_pairs={{8,0},{16,8},{24,16},{32,24},{40,32},{48,40},{56,48},{64,56},{72,6... | collective-permute-start | bytes 1105928 | tf_op jit(solution)/shard_map/ppermute | solution.py:17
  47.0 2.1 collective-permute-start
  50.1 8.0 %collective-permute-done.1 = bf16[1,96,1920]{2,1,0:T(8,128)(2,1)S(1)} collective-permute-done((bf16[1,96,1920]{2,1,0:T(8,128)(2,1)S(1)}, bf16[1,96,1920]{2,1,0:T(8,128)(2,1)S(1)}, u32[]{:S(2)}, u32[]{:S(2)}) %collective-permute-start.1) | collective-permute-done | bytes 368672 | tf_op jit(solution)/shard_map/ppermute | solution.py:17
  58.1 3.4 collective-permute-done
  65.6 2.8 fusion.90
  68.5 71.6 %all-gather.7.cloned.1.call-done = bf16[32,60,3456]{2,1,0:T(8,128)(2,1)} async-done(((bf16[1,60,3456]{2,1,0:T(8,128)(2,1)}), bf16[32,60,3456]{2,1,0:T(8,128)(2,1)}) %all-gather.7.cloned.1.call-update) | async-done | bytes 13271056 | tf_op jit(solution)/shard_map/all_gather | solution.py:78
  140.1 43.6 %copy.38 = bf16[32,60,3456]{1,0,2:T(8,128)(2,1)} copy(bf16[32,60,3456]{2,1,0:T(8,128)(2,1)} %all-gather.7.cloned.1.call-done) | data formatting | bytes 26542080 | tf_op jit(solution)/shard_map/all_gather | solution.py:78
  183.7 72.5 %reshape.150 = bf16[1920,192,2,3,3]{0,4,3,2,1:T(4,128)(2,1)} reshape(bf16[32,60,3456]{1,0,2:T(8,128)(2,1)} %copy.38) | data formatting | bytes 26542080 | tf_op jit(solution)/shard_map/reshape | solution.py:40
  256.2 10.0 %copy.39 = bf16[3,3,1920,2,192]{2,4,3,1,0:T(8,128)(2,1)S(1)} copy(bf16[3,3,1920,2,192]{2,1,0,3,4:T(4,128)(2,1)} %bitcast.211) | data formatting | bytes 26542080 | tf_op jit(solution)/shard_map/transpose | solution.py:40
  280.3 16.7 %all_gather.27 = bf16[3,96,1536]{1,0,2:T(4,128)(2,1)} all-gather(bf16[3,96,192]{1,0,2:T(4,128)(2,1)S(1)} %copy.41), channel_id=1, replica_groups=mesh['space'=32,'chan'=8] {'chan'}, dimensions={2}, use_global_device_ids=true | all-gather | bytes 995328 | tf_op jit(solution)/shard_map/all_gather | solution.py:63
  297.0 2.6 copy.42
  300.4 3.6 collective-permute-start.3
  304.1 1.9 collective-permute-start.2
  306.0 14.4 %all-gather.1 = bf16[1,3,96,384]{2,3,1,0:T(8,128)(2,1)} all-gather(bf16[1,3,96,48]{2,3,1,0:T(8,128)(2,1)S(1)} %copy-done.20), channel_id=3, replica_groups=mesh['space'=32,'chan'=8] {'chan'}, dimensions={3}, use_global_device_ids=true | all-gather | bytes 248832 | tf_op jit(solution)/shard_map/all_gather | solution.py:54
  321.7 40.5 %copy.45 = bf16[32,30,3456]{1,0,2:T(8,128)(2,1)} copy(bf16[32,30,3456]{2,1,0:T(8,128)(2,1)} %all-gather.9.cloned.1.call-done) | data formatting | bytes 13271040 | tf_op jit(solution)/shard_map/all_gather | solution.py:79
  362.1 52.5 %reshape.164 = bf16[960,192,2,3,3]{0,4,3,2,1:T(4,128)(2,1)} reshape(bf16[32,30,3456]{1,0,2:T(8,128)(2,1)} %copy.45) | data formatting | bytes 13271040 | tf_op jit(solution)/shard_map/reshape | solution.py:45
  414.7 31.8 %copy.46 = bf16[3,3,960,2,192]{4,3,2,1,0:T(2,128)(2,1)} copy(bf16[3,3,960,2,192]{2,1,0,3,4:T(4,128)(2,1)} %bitcast.212) | data formatting | bytes 13271040 | tf_op jit(solution)/shard_map/transpose | solution.py:45
  446.4 18.9 %reshape.165 = bf16[3,3,1920,192]{3,2,1,0:T(8,128)(2,1)} reshape(bf16[3,3,960,2,192]{4,3,2,1,0:T(2,128)(2,1)} %copy.46) | data formatting | bytes 13271040 | tf_op jit(solution)/shard_map/reshape | solution.py:45
  476.1 15.2 %all_gather.30 = bf16[3,96,1536]{1,0,2:T(4,128)(2,1)S(1)} all-gather(bf16[3,96,192]{1,0,2:T(4,128)(2,1)S(1)} %copy.50), channel_id=1, replica_groups=mesh['space'=32,'chan'=8] {'chan'}, dimensions={2}, use_global_device_ids=true | all-gather | bytes 995328 | tf_op jit(solution)/shard_map/all_gather | solution.py:55
  492.3 5.7 collective-permute-start.5
  498.0 2.2 collective-permute-start.4
  500.2 5.6 collective-permute-done.5
  505.8 5.9 %collective-permute-done.4 = bf16[1,96,1920]{2,1,0:T(8,128)(2,1)S(1)} collective-permute-done((bf16[1,96,1920]{2,1,0:T(8,128)(2,1)S(1)}, bf16[1,96,1920]{2,1,0:T(8,128)(2,1)S(1)}, u32[]{:S(2)}, u32[]{:S(2)}) %collective-permute-start.4) | collective-permute-done | bytes 368672 | tf_op jit(solution)/shard_map/ppermute | solution.py:14
  512.9 3.2 fusion.22
  525.4 16.6 %all_gather.31 = bf16[3,96,1536]{1,0,2:T(4,128)(2,1)} all-gather(bf16[3,96,192]{1,0,2:T(4,128)(2,1)S(1)} %copy.52), channel_id=1, replica_groups=mesh['space'=32,'chan'=8] {'chan'}, dimensions={2}, use_global_device_ids=true | all-gather | bytes 995328 | tf_op jit(solution)/shard_map/all_gather | solution.py:63
  542.0 2.6 copy.53
  545.5 1.9 collective-permute-start.7
  547.4 3.4 collective-permute-start.6
  553.4 2.7 collective-permute-done.7
  556.1 4.0 collective-permute-done.6
  (145 shorter events, 61.9 us)
Async XLA Ops:
  6.5 133.5 %all-gather.7.cloned.1.call-start = ((), (), s32[]{:S(2)}) async-start(), calls=%async_computation | async-start | bytes 14598144 | tf_op jit(solution)/shard_map/all_gather | solution.py:78
  7.3 314.4 %all-gather.9.cloned.1.call-start = ((), (), s32[]{:S(2)}) async-start(), calls=%async_computation.1 | async-start | bytes 7299072 | tf_op jit(solution)/shard_map/all_gather | solution.py:79
  38.9 11.1 %copy-start.22 = (f32[2,192]{1,0:T(2,128)S(1)}, f32[2,192]{1,0:T(2,128)}, u32[]{:S(2)}) copy-start(f32[2,192]{1,0:T(2,128)} %param.9) | copy-start | bytes 4612
  39.2 18.9 %collective-permute-start.1 = (bf16[1,96,1920]{2,1,0:T(8,128)(2,1)S(1)}, bf16[1,96,1920]{2,1,0:T(8,128)(2,1)S(1)}, u32[]{:S(2)}, u32[]{:S(2)}) collective-permute-start(bf16[1,96,1920]{2,1,0:T(8,128)(2,1)S(1)} %get-tuple-element.44), channel_id=1, source_target_pairs={{8,0},{16,8},{24,16},{32,24},{40,32},{48,40},{56,48},{64,56},{72,6... | collective-permute-start | bytes 1105928 | tf_op jit(solution)/shard_map/ppermute | solution.py:17
  47.0 14.6 %collective-permute-start = (bf16[1,96,1920]{2,1,0:T(8,128)(2,1)S(1)}, bf16[1,96,1920]{2,1,0:T(8,128)(2,1)S(1)}, u32[]{:S(2)}, u32[]{:S(2)}) collective-permute-start(bf16[1,96,1920]{2,1,0:T(8,128)(2,1)S(1)} %get-tuple-element.43), channel_id=1, source_target_pairs={{0,8},{8,16},{16,24},{24,32},{32,40},{40,48},{48,56},{56,64},{64,7... | collective-permute-start | bytes 1105928 | tf_op jit(solution)/shard_map/ppermute | solution.py:14
  65.6 256.0 %copy-start = (bf16[5,98,1920]{2,1,0:T(8,128)(2,1)}, bf16[5,98,1920]{2,1,0:T(8,128)(2,1)S(1)}, u32[]{:S(2)}) copy-start(bf16[5,98,1920]{2,1,0:T(8,128)(2,1)S(1)} %select_maximum_fusion.3) | copy-start | bytes 5644804
  256.2 10.0 %copy-start.17 = (bf16[3,96,1920]{2,1,0:T(8,128)(2,1)S(1)}, bf16[3,96,1920]{2,1,0:T(8,128)(2,1)}, u32[]{:S(2)}) copy-start(bf16[3,96,1920]{2,1,0:T(8,128)(2,1)} %get-tuple-element.30) | copy-start | bytes 3317764
  266.2 12.0 %copy-start.2 = (bf16[3,3,1920,2,192]{2,4,3,1,0:T(8,128)(2,1)}, bf16[3,3,1920,2,192]{2,4,3,1,0:T(8,128)(2,1)S(1)}, u32[]{:S(2)}) copy-start(bf16[3,3,1920,2,192]{2,4,3,1,0:T(8,128)(2,1)S(1)} %copy.39) | copy-start | bytes 39813124
  266.2 2.1 copy-start.13
  268.3 2.1 copy-start.16
  270.4 2.1 copy-start.12
  272.5 1.2 copy-start.15
  273.7 1.2 copy-start.14
  297.0 9.0 %copy-start.20 = (bf16[1,3,96,48]{2,3,1,0:T(8,128)(2,1)S(1)}, bf16[1,3,96,48]{2,3,1,0:T(8,128)(2,1)}, u32[]{:S(2)}) copy-start(bf16[1,3,96,48]{2,3,1,0:T(8,128)(2,1)} %get-tuple-element.51) | copy-start | bytes 82948
  300.4 164.9 %collective-permute-start.3 = (bf16[1,96,1536]{2,1,0:T(8,128)(2,1)}, bf16[1,96,1536]{2,1,0:T(8,128)(2,1)}, u32[]{:S(2)}, u32[]{:S(2)}) collective-permute-start(bf16[1,96,1536]{2,1,0:T(8,128)(2,1)} %get-tuple-element.48), channel_id=1, source_target_pairs={{8,0},{16,8},{24,16},{32,24},{40,32},{48,40},{56,48},{64,56},{72,6... | collective-permute-start | bytes 884744 | tf_op jit(solution)/shard_map/ppermute | solution.py:17
  304.1 161.2 %collective-permute-start.2 = (bf16[1,96,1536]{2,1,0:T(8,128)(2,1)}, bf16[1,96,1536]{2,1,0:T(8,128)(2,1)}, u32[]{:S(2)}, u32[]{:S(2)}) collective-permute-start(bf16[1,96,1536]{2,1,0:T(8,128)(2,1)} %get-tuple-element.47), channel_id=1, source_target_pairs={{0,8},{8,16},{16,24},{24,32},{32,40},{40,48},{48,56},{56,64},{64,7... | collective-permute-start | bytes 884744 | tf_op jit(solution)/shard_map/ppermute | solution.py:14
  465.3 1.5 slice-start
  466.8 3.5 copy-start.3
  492.3 13.5 %collective-permute-start.5 = (bf16[1,96,1920]{2,1,0:T(8,128)(2,1)S(1)}, bf16[1,96,1920]{2,1,0:T(8,128)(2,1)S(1)}, u32[]{:S(2)}, u32[]{:S(2)}) collective-permute-start(bf16[1,96,1920]{2,1,0:T(8,128)(2,1)S(1)} %get-tuple-element.39), channel_id=1, source_target_pairs={{8,0},{16,8},{24,16},{32,24},{40,32},{48,40},{56,48},{64,56},{72,6... | collective-permute-start | bytes 1105928 | tf_op jit(solution)/shard_map/ppermute | solution.py:17
  498.0 13.7 %collective-permute-start.4 = (bf16[1,96,1920]{2,1,0:T(8,128)(2,1)S(1)}, bf16[1,96,1920]{2,1,0:T(8,128)(2,1)S(1)}, u32[]{:S(2)}, u32[]{:S(2)}) collective-permute-start(bf16[1,96,1920]{2,1,0:T(8,128)(2,1)S(1)} %get-tuple-element.38), channel_id=1, source_target_pairs={{0,8},{8,16},{16,24},{24,32},{32,40},{40,48},{48,56},{56,64},{64,7... | collective-permute-start | bytes 1105928 | tf_op jit(solution)/shard_map/ppermute | solution.py:14
  511.7 4.7 slice-start.2
  512.2 41.2 %copy-start.1 = (bf16[5,98,1920]{2,1,0:T(8,128)(2,1)}, bf16[5,98,1920]{2,1,0:T(8,128)(2,1)S(1)}, u32[]{:S(2)}) copy-start(bf16[5,98,1920]{2,1,0:T(8,128)(2,1)S(1)} %select_maximum_fusion) | copy-start | bytes 5644804
  512.2 4.1 slice-start.3
  512.3 4.7 slice-start.4
  512.9 5.1 slice-start.5
  523.5 1.6 copy-start.7
  542.0 23.0 %slice-start.6 = ((s8[8847360]{0:T(1024)(128)(4,1)}), s8[458752]{0:T(1024)(128)(4,1)S(1)}, s32[]{:S(2)}) async-start(s8[8847360]{0:T(1024)(128)(4,1)} %bitcast.233), calls=%async_computation.8 | async-start | bytes 917504
  545.5 10.6 %collective-permute-start.7 = (bf16[1,96,1536]{2,1,0:T(8,128)(2,1)}, bf16[1,96,1536]{2,1,0:T(8,128)(2,1)}, u32[]{:S(2)}, u32[]{:S(2)}) collective-permute-start(bf16[1,96,1536]{2,1,0:T(8,128)(2,1)} %get-tuple-element.46), channel_id=1, source_target_pairs={{8,0},{16,8},{24,16},{32,24},{40,32},{48,40},{56,48},{64,56},{72,6... | collective-permute-start | bytes 884744 | tf_op jit(solution)/shard_map/ppermute | solution.py:17
  547.4 12.7 %collective-permute-start.6 = (bf16[1,96,1536]{2,1,0:T(8,128)(2,1)}, bf16[1,96,1536]{2,1,0:T(8,128)(2,1)}, u32[]{:S(2)}, u32[]{:S(2)}) collective-permute-start(bf16[1,96,1536]{2,1,0:T(8,128)(2,1)} %get-tuple-element.45), channel_id=1, source_target_pairs={{0,8},{8,16},{16,24},{24,32},{32,40},{40,48},{48,56},{56,64},{64,7... | collective-permute-start | bytes 884744 | tf_op jit(solution)/shard_map/ppermute | solution.py:14
  553.4 8.2 %slice-start.1 = ((bf16[5,98,1920]{2,1,0:T(8,128)(2,1)}), bf16[5,98,384]{2,1,0:T(8,128)(2,1)S(1)}, s32[]{:S(2)}) async-start(bf16[5,98,1920]{2,1,0:T(8,128)(2,1)} %copy-done.1), calls=%async_computation.3 | async-start | bytes 798720 | tf_op jit(solution)/shard_map/slice | solution.py:94
  553.4 11.6 %slice-start.7 = ((s8[8847360]{0:T(1024)(128)(4,1)}), s8[4194304]{0:T(1024)(128)(4,1)S(1)}, s32[]{:S(2)}) async-start(s8[8847360]{0:T(1024)(128)(4,1)} %bitcast.233), calls=%async_computation.9 | async-start | bytes 8388608
  561.6 3.5 slice-start.8
  (11 other events, 10.4 us)
Sparse Core Ops, SparseCore 0:
  9.9 130.1 all-gather.6
  142.7 89.0 all-gather.8
where the time goes:
time: 588 us; the launch traced here: 578 us
  local copies, waits for them, and re-layouts  303 us (52%)
  waiting for transfers between devices  103 us (18%)
  blocking collectives  91.1 us (15%)
  starting transfers between devices  28.6 us (5%)
  matrix products  26.2 us (4%)
  between operations  14.6 us (2%)
  other arithmetic  11.9 us (2%)
    reshape x1, local copies, waits for them, and re-layouts, gate_taps(): raw.reshape(count, own, 2, 3, 3).transpose(3, 4, 0, 2, 1)  72.5 us
    all_gather x1, waiting for transfers between devices, local(): lax.all_gather(gate_weight, 'space', axis=0, tiled=True)  71.6 us
    reshape x2, local copies, waits for them, and re-layouts, cand_taps(): raw.reshape(count, own, 2, 3, 3).transpose(3, 4, 0, 2, 1)  71.4 us
    all_gather x1, local copies, waits for them, and re-layouts, local(): lax.all_gather(gate_weight, 'space', axis=0, tiled=True)  43.6 us
    all_gather x1, local copies, waits for them, and re-layouts, local(): lax.all_gather(cand_weight, 'space', axis=0, tiled=True)  40.5 us
    all_gather x2, blocking collectives, gather_gated(): gated_full = lax.all_gather(gated, 'chan', axis=2, tiled=True)  33.3 us
    transpose x1, local copies, waits for them, and re-layouts, cand_taps(): raw.reshape(count, own, 2, 3, 3).transpose(3, 4, 0, 2, 1)  31.8 us
    all_gather x2, blocking collectives, gather_inputs(): lax.all_gather(state_now, 'chan', axis=2, tiled=True)  30.5 us
  transfers between devices with their start and end apart: 10, of which 7 were waited for; matrix products, arithmetic and copies ran while one was open for 51% of the time, Pallas kernels for 0%

commit v1 on v0

v1 whole, which is shorter than its diff:
```python
import functools

import jax
import jax.numpy as jnp
from jax import lax
from jax.experimental import pallas as pl
from jax.experimental.pallas import tpu as pltpu
from jax.sharding import PartitionSpec as P

W = 96
ROWS = 3
CELLS = ROWS * W
HALO = (ROWS + 2) * W
OWN = 192
COND = 48
SHARD = 60
SLOT = 64
WIN = 256
BF = jnp.bfloat16
F32 = jnp.float32
PAIRS = tuple(
    (t, n)
    for t in range(1, 8)
    for n in range(8)
    if max(240 * t, 384 + 192 * n) < min(240 * t + 240, 576 + 192 * n)
)


def gate_taps(raw):
    taps = raw.reshape(30, 2, OWN, 2, 9).transpose(4, 1, 0, 3, 2)
    taps = jnp.pad(taps, ((0, 0), (0, 0), (0, 2), (0, 0), (0, 0)))
    return taps.reshape(9, SLOT, 2 * OWN)


def cand_taps(raw):
    taps = raw.reshape(30, OWN, 2, 9).transpose(3, 2, 0, 1)
    taps = jnp.pad(taps, ((0, 0), (0, 0), (0, 2), (0, 0)))
    return taps.reshape(9, SLOT, OWN)


def kernel(
    act_ref, wg_ref, wc_ref, bias_ref, out_ref,
    init, gbuf0, sbuf, gbuf1, wg, wc, xs, emat, acc, cacc, upd, prev,
    gated, fresh, landed, sib_bias,
    xsend, xrecv, wsend, wz, wl, wr, wo, wd, osem, orecv, bsem,
):
    s = lax.axis_index("space")
    ch = lax.axis_index("chan")
    x, z = s // 8, s % 8
    b, y, c = z % 2, ch // 2, ch % 2
    job_row = s - b + c
    job_chan = 2 * y + b
    right = (x + 1) % 4
    left = (x + 3) % 4
    opposite = (x + 2) % 4

    barrier = pltpu.get_barrier_semaphore()

    def greet(space, chan):
        pl.semaphore_signal(
            barrier, inc=1, device_id=(space, chan), device_id_type=pl.DeviceIdType.MESH
        )

    def greet_line(i, carry):
        space, chan = 8 * x + i // 8, i % 8

        @pl.when(jnp.logical_or(space != s, chan != ch))
        def _():
            greet(space, chan)

        return carry

    lax.fori_loop(0, 64, greet_line, 0)
    greet(8 * right + z, ch)
    greet(8 * left + z, ch)

    @pl.when(z < 2)
    def _():
        lax.fori_loop(0, 16, lambda i, k: (greet(8 * left + 6 + i // 8, i % 8), k)[1], 0)

    @pl.when(z >= 6)
    def _():
        lax.fori_loop(0, 16, lambda i, k: (greet(8 * right + i // 8, i % 8), k)[1], 0)

    at_end = jnp.logical_or(z < 2, z >= 6)
    pl.semaphore_wait(barrier, 65 + 16 * at_end.astype(jnp.int32))

    def remote(src, dst, send, recv, space, chan):
        return pltpu.make_async_remote_copy(
            src_ref=src, dst_ref=dst, send_sem=send, recv_sem=recv,
            device_id=(space, chan), device_id_type=pl.DeviceIdType.MESH,
        )

    def push(src, dst, send, recv, space, chan):
        mine = jnp.logical_and(space == s, chan == ch)

        @pl.when(mine)
        def _():
            pltpu.make_async_copy(src, dst, recv).start()

        @pl.when(jnp.logical_not(mine))
        def _():
            remote(src, dst, send, recv, space, chan).start()

    def sent(src, dst, send, recv, space, chan):
        mine = jnp.logical_and(space == s, chan == ch)

        @pl.when(jnp.logical_not(mine))
        def _():
            remote(src, dst, send, recv, space, chan).wait_send()

    def arrived(dst, recv):
        pltpu.make_async_copy(dst, dst, recv).wait()

    def exchange(act, k, row, chan, src, buf):
        def one(i, carry):
            kind, p = i // 8, i % 8
            to_row = (row + jnp.where(kind == 0, 0, jnp.where(kind == 1, 1, 31))) % 32
            space = to_row - to_row % 2 + p % 2
            dest = p - p % 2 + to_row % 2

            @pl.when(kind == 0)
            def _():
                act(src, buf.at[chan, pl.ds(W, CELLS)], xsend.at[i], xrecv.at[k, 0, chan], space, dest)

            @pl.when(kind == 1)
            def _():
                act(src.at[pl.ds(2 * W, W)], buf.at[chan, pl.ds(0, W)], xsend.at[i],
                    xrecv.at[k, 1, chan], space, dest)

            @pl.when(kind == 2)
            def _():
                act(src.at[pl.ds(0, W)], buf.at[chan, pl.ds(4 * W, W)], xsend.at[i],
                    xrecv.at[k, 2, chan], space, dest)

            return carry

        lax.fori_loop(0, 24, one, 0)

    def exchanged(k, buf):
        def one(n, carry):
            arrived(buf.at[n, pl.ds(W, CELLS)], xrecv.at[k, 0, n])
            arrived(buf.at[n, pl.ds(0, W)], xrecv.at[k, 1, n])
            arrived(buf.at[n, pl.ds(4 * W, W)], xrecv.at[k, 2, n])
            return carry

        lax.fori_loop(0, 8, one, 0)

    group = z // 4
    spot = z % 4
    mine = ((wg_ref, wg), (wc_ref, wc))

    def kernel_z(kind, act):
        src, buf = mine[kind]

        def one(i, carry):
            act(src, buf.at[2 * x + group, :, spot], wsend.at[kind, i], wz.at[kind, spot],
                8 * x + 2 * i + c, 2 * y + group)
            return carry

        lax.fori_loop(0, 4, one, 0)

    here, lower, upper, across = 2 * x + c, 2 * left + c, 2 * right + c, 2 * opposite + c

    def hop(kind, t, i, send, recv, space, chan):
        buf = mine[kind][1]
        return remote(buf.at[t, :, i], buf.at[t, :, i], wsend.at[kind, send], recv, space, chan)

    def go_right(kind, i):
        return hop(kind, here, i, 4 + i, wl.at[kind, i], 8 * right + z, ch)

    def go_left(kind, i):
        return hop(kind, here, i, 8 + i, wr.at[kind, i], 8 * left + z, ch)

    def pass_right(kind, i):
        return hop(kind, lower, i, 12 + i, wo.at[kind, i], 8 * right + z, ch)

    def pass_left(kind, i):
        return hop(kind, upper, i, 12 + i, wo.at[kind, i], 8 * left + z, ch)

    def share(kind, j, i):
        t = (here, lower, upper, across)[j]
        return hop(kind, t, i, 16 + 4 * j + i, wd.at[kind, j, i], s, 2 * y + 1 - c)

    def piece(kind, t, i):
        return mine[kind][1].at[t, :, i]

    def kernel_own(kind):
        for i in range(4):
            arrived(piece(kind, here, i), wz.at[kind, i])
            go_right(kind, i).start()
            go_left(kind, i).start()
            share(kind, 0, i).start()

    def kernel_sides(kind):
        for i in range(4):
            arrived(piece(kind, lower, i), wl.at[kind, i])
            if i % 2 == 0:
                pass_right(kind, i).start()
            share(kind, 1, i).start()
            arrived(piece(kind, upper, i), wr.at[kind, i])
            if i % 2 == 1:
                pass_left(kind, i).start()
            share(kind, 2, i).start()

    def kernel_across(kind):
        for i in range(4):
            arrived(piece(kind, across, i), wo.at[kind, i])
            share(kind, 3, i).start()

    def kernel_shared(kind, j):
        t = 2 * ((here, lower, upper, across)[j] // 2) + 1 - c
        for i in range(4):
            arrived(piece(kind, t, i), wd.at[kind, j, i])
        return t

    def kernel_sent(kind):
        kernel_z(kind, sent)
        for i in range(4):
            go_right(kind, i).wait_send()
            go_left(kind, i).wait_send()
            if i % 2 == 0:
                pass_right(kind, i).wait_send()
            else:
                pass_left(kind, i).wait_send()
            for j in range(4):
                share(kind, j, i).wait_send()

    def slot_channel(t, rows):
        j = lax.broadcasted_iota(jnp.int32, (rows, WIN), 1)
        r = j % SLOT
        m = r % 32
        k = SHARD * (4 * t + j // SLOT) + 2 * m + r // 32
        return jnp.where(m < 30, k, -1)

    def spread(t, v):
        cell = lax.broadcasted_iota(jnp.int32, (HALO, WIN), 0)
        col = cell % W
        inside = jnp.logical_and(
            jnp.logical_or(cell >= W, job_row > 0),
            jnp.logical_or(cell < 4 * W, job_row < 31),
        )
        v = jnp.where(inside, v, 0.0)
        low = jnp.where(col == 0, 0.0, pltpu.roll(v, 1, 0))
        high = jnp.where(col == W - 1, 0.0, pltpu.roll(v, HALO - 1, 0))
        xs[:, 768 * t:768 * t + 256] = low.astype(BF)
        xs[:, 768 * t + 256:768 * t + 512] = v.astype(BF)
        xs[:, 768 * t + 512:768 * t + 768] = high.astype(BF)

    def cond_slots(step, t):
        v = jnp.zeros((HALO, WIN), F32)
        lane = lax.broadcasted_iota(jnp.int32, (128, WIN), 0)
        want = slot_channel(t, 128)
        for n in range(5 * t, min(8, 5 * t + 5)):
            here_n = jnp.logical_and(lane >= COND * step, lane < COND * step + COND)
            hit = jnp.logical_and(here_n, want == COND * n + lane - COND * step)
            e = hit.astype(F32).astype(BF)
            v = v + jnp.dot(init[n, :, 0:128], e, preferred_element_type=F32)
        return v

    def build(step, buf, base, first):
        if first:
            spread(0, cond_slots(step, 0))
        for t in range(1, 8):
            v = cond_slots(step, 1) if t == 1 else jnp.zeros((HALO, WIN), F32)
            for q, (pt, n) in enumerate(PAIRS):
                if pt == t:
                    v = v + jnp.dot(buf[n, :, base:base + OWN], emat[q], preferred_element_type=F32)
            spread(t, v)

    def window(buf, total, t):
        lane = pl.multiple_of(768 * t, 768)
        out = total.shape[1]
        for a in range(3):
            total[...] += jnp.dot(
                xs[pl.ds(a * W, CELLS), pl.ds(lane, 768)],
                buf[t, 3 * a:3 * a + 3].reshape(768, out),
                preferred_element_type=F32,
            )

    def bias(row):
        return jnp.where(b == c, bias_ref[row:row + 1, 0:OWN], sib_bias[row:row + 1, 0:OWN])

    def finish_gate(k):
        pre = acc[...]
        upd[...] = jax.nn.sigmoid(pre[:, :OWN] + bias(0))
        reset = jax.nn.sigmoid(pltpu.roll(pre, OWN, 1)[:, :OWN] + bias(1))
        gated[k] = (reset * prev[...]).astype(BF)

    def finish_cand(k):
        candidate = jnp.tanh(cacc[...] + bias(2))
        u = upd[...]
        new = ((1.0 - u) * prev[...] + u * candidate).astype(BF)
        fresh[k] = new
        prev[...] = new.astype(F32)

    def deliver(k, act):
        act(fresh.at[k], landed.at[k], osem.at[k], orecv.at[k], job_row, job_chan)

    exchange(push, 0, s, ch, act_ref, init)
    bias_copy = remote(bias_ref, sib_bias, bsem.at[0], bsem.at[1], s, 2 * y + 1 - c)
    bias_copy.start()
    kernel_z(0, push)
    kernel_z(1, push)
    for q, (t, n) in enumerate(PAIRS):
        lane = lax.broadcasted_iota(jnp.int32, (OWN, WIN), 0)
        hit = slot_channel(t, OWN) == 384 + 192 * n + lane
        emat[q] = hit.astype(F32).astype(BF)
    acc[...] = jnp.zeros_like(acc)
    cacc[...] = jnp.zeros_like(cacc)
    kernel_own(0)
    exchanged(0, init)
    exchange(sent, 0, s, ch, act_ref, init)
    bias_copy.wait()
    prev[...] = init[job_chan, pl.ds(W, CELLS), 128:128 + OWN].astype(F32)
    build(0, init, 128, True)

    window(wg, acc, here)
    kernel_sides(0)
    kernel_own(1)

    def shared_window(kind, buf, total, j):
        window(buf, total, kernel_shared(kind, j))

    window(wg, acc, lower)
    window(wg, acc, upper)
    shared_window(0, wg, acc, 0)
    shared_window(0, wg, acc, 1)
    shared_window(0, wg, acc, 2)
    kernel_across(0)
    window(wg, acc, across)
    shared_window(0, wg, acc, 3)
    finish_gate(0)
    exchange(push, 1, job_row, job_chan, gated.at[0], gbuf0)
    kernel_sides(1)
    exchanged(1, gbuf0)
    exchange(sent, 1, job_row, job_chan, gated.at[0], gbuf0)
    build(0, gbuf0, 0, False)
    window(wc, cacc, here)
    window(wc, cacc, lower)
    window(wc, cacc, upper)
    shared_window(1, wc, cacc, 0)
    shared_window(1, wc, cacc, 1)
    shared_window(1, wc, cacc, 2)
    kernel_across(1)
    window(wc, cacc, across)
    shared_window(1, wc, cacc, 3)
    finish_cand(0)

    exchange(push, 2, job_row, job_chan, fresh.at[0], sbuf)
    deliver(0, push)
    acc[...] = jnp.zeros_like(acc)
    cacc[...] = jnp.zeros_like(cacc)
    exchanged(2, sbuf)
    exchange(sent, 2, job_row, job_chan, fresh.at[0], sbuf)
    build(1, sbuf, 0, True)

    def all_windows(buf, total):
        def one(t, carry):
            window(buf, total, t)
            return carry

        lax.fori_loop(0, 8, one, 0)

    all_windows(wg, acc)
    finish_gate(1)
    exchange(push, 3, job_row, job_chan, gated.at[1], gbuf1)
    kernel_sent(0)
    kernel_sent(1)
    exchanged(3, gbuf1)
    exchange(sent, 3, job_row, job_chan, gated.at[1], gbuf1)
    build(1, gbuf1, 0, False)
    all_windows(wc, cacc)
    finish_cand(1)
    deliver(1, push)
    for k in range(2):
        arrived(landed.at[k], orecv.at[k])
        out_ref[k] = landed[k]
        deliver(k, sent)


def local(hidden, conditioning, gate_weight, gate_bias, cand_weight, cand_bias):
    state = hidden.reshape(ROWS, OWN, W).transpose(0, 2, 1).reshape(CELLS, OWN)
    cond = conditioning.reshape(2, ROWS, COND, W).transpose(1, 3, 0, 2).reshape(CELLS, 2 * COND)
    act = jnp.concatenate(
        [cond, jnp.zeros((CELLS, 32), BF), state, jnp.zeros((CELLS, 64), BF)], axis=1
    )
    bias = jnp.concatenate([gate_bias, cand_bias[None]], axis=0)
    bias = jnp.pad(bias, ((0, 5), (0, 64)))
    vmem = pl.BlockSpec(memory_space=pltpu.VMEM)
    dma = pltpu.SemaphoreType.DMA
    out = pl.pallas_call(
        kernel,
        out_shape=jax.ShapeDtypeStruct((2, CELLS, OWN), BF),
        in_specs=[vmem] * 4,
        out_specs=vmem,
        scratch_shapes=[
            pltpu.VMEM((8, HALO, 384), BF),
            pltpu.VMEM((8, HALO, OWN), BF),
            pltpu.VMEM((8, HALO, OWN), BF),
            pltpu.VMEM((8, HALO, OWN), BF),
            pltpu.VMEM((8, 9, 4, SLOT, 2 * OWN), BF),
            pltpu.VMEM((8, 9, 4, SLOT, OWN), BF),
            pltpu.VMEM((HALO, 8 * 768), BF),
            pltpu.VMEM((len(PAIRS), OWN, WIN), BF),
            pltpu.VMEM((CELLS, 2 * OWN), F32),
            pltpu.VMEM((CELLS, OWN), F32),
            pltpu.VMEM((CELLS, OWN), F32),
            pltpu.VMEM((CELLS, OWN), F32),
            pltpu.VMEM((2, CELLS, OWN), BF),
            pltpu.VMEM((2, CELLS, OWN), BF),
            pltpu.VMEM((2, CELLS, OWN), BF),
            pltpu.VMEM((8, 256), F32),
            dma((24,)),
            dma((4, 3, 8)),
            dma((2, 32)),
            dma((2, 4)),
            dma((2, 4)),
            dma((2, 4)),
            dma((2, 4)),
            dma((2, 4, 4)),
            dma((2,)),
            dma((2,)),
            dma((2,)),
        ],
        compiler_params=pltpu.CompilerParams(
            collective_id=0, has_side_effects=True, vmem_limit_bytes=63 * 1024 * 1024
        ),
    )(act, gate_taps(gate_weight), cand_taps(cand_weight), bias)
    frames = out.reshape(2, ROWS, W, OWN).transpose(0, 1, 3, 2)
    return frames.reshape(2, ROWS, OWN * W)


def solution(mesh):
    placed = (
        P("space", "chan"),
        P(None, "space", "chan"),
        P("space", "chan"),
        P(None, "chan"),
        P("space", "chan"),
        P("chan"),
    )
    return jax.shard_map(
        local, mesh=mesh, in_specs=placed, out_specs=P(None, "space", "chan"), check_vma=False
    )
```

time: 588 us -> 320 us (0.54); the launches traced: 578 us -> 320 us
  Pallas kernels: 0 us -> 279 us
  local copies, waits for them, and re-layouts: 303 us -> 39 us
  waiting for transfers between devices: 103 us -> 0 us
  blocking collectives: 91.1 us -> 0 us
  starting transfers between devices: 28.6 us -> 0 us
  matrix products: 26.2 us -> 0 us
  between operations: 14.6 us -> 0.13 us
  other arithmetic: 11.9 us -> 1.37 us
    pallas_call x0 -> x1, Pallas kernels: none -> 279 us  [local(): pl.pallas_call(kernel, out_shape=jax.ShapeDtypeStruct((2, CELLS, OWN), BF...]
    reshape x11 -> x10, local copies, waits for them, and re-layouts: 147 us -> 21.7 us  [the longest x1 18.3 us: gate_taps(): taps = raw.reshape(30, 2, OWN, 2, 9).transpose(4, 1, 0, 3, 2)]
    all_gather x8 -> x0, local copies, waits for them, and re-layouts: 92.3 us -> none  [the longest x1 43.6 us: local(): lax.all_gather(gate_weight, 'space', axis=0, tiled=True)]
    all_gather x6 -> x0, blocking collectives: 91.1 us -> none  [the longest x2 33.3 us: gather_gated(): gated_full = lax.all_gather(gated, 'chan', axis=2, tiled=True)]
    all_gather x2 -> x0, waiting for transfers between devices: 71.6 us -> none  [the longest x1 71.6 us: local(): lax.all_gather(gate_weight, 'space', axis=0, tiled=True)]
    transpose x3 -> x1, local copies, waits for them, and re-layouts: 41.9 us -> 1.15 us  [local(): frames = out.reshape(2, ROWS, W, OWN).transpose(0, 1, 3, 2)]
    ppermute x8 -> x0, waiting for transfers between devices: 29.7 us -> none  [the longest x4 16.3 us: with_halo(): lax.ppermute(lax.slice_in_dim(block, 0, width, axis=dim), axis, backward)]
    ppermute x8 -> x0, starting transfers between devices: 28.6 us -> none  [the longest x4 19 us: with_halo(): lax.ppermute(lax.slice_in_dim(block, 0, width, axis=dim), axis, backward)]
  transfers between devices with their start and end apart: 10 -> 0, of which waited for: 7 -> 0; matrix products, arithmetic and copies ran while one was open for 51% -> 0% of each run, Pallas kernels for 0% -> 0%
where the time goes in v1:
time: 320 us
  Pallas kernels  279 us (87%)
  local copies, waits for them, and re-layouts  39 us (12%)
    pallas_call x1, Pallas kernels, local(): pl.pallas_call(kernel, out_shape=jax.ShapeDtypeStruct((2, CELLS, OWN), BF...  279 us
    reshape x1, local copies, waits for them, and re-layouts, gate_taps(): taps = raw.reshape(30, 2, OWN, 2, 9).transpose(4, 1, 0, 3, 2)  18.3 us
    unnamed x13, local copies, waits for them, and re-layouts  14.7 us

profile of v1, /device:TPU:31, one launch (start us, length us, event | category | flops | bytes accessed | tf_op | source)
XLA Modules:
  0.0 319.5 jit_solution(10882219545402945485)
XLA Ops:
  0.0 18.3 %reshape.34 = bf16[30,2,192,2,9]{4,3,2,1,0:T(2,128)(2,1)} reshape(bf16[60,3456]{1,0:T(8,128)(2,1)} %param.8) | data formatting | bytes 829440 | tf_op jit(solution)/shard_map/reshape | solution.py:30
  18.3 0.0 copy-start
  18.3 0.0 copy-start.2
  18.3 13.2 %copy.19 = bf16[9,2,30,2,192]{4,3,2,1,0:T(2,128)(2,1)S(1)} copy(bf16[9,2,30,2,192]{0,3,4,1,2:T(2,128)(2,1)} %bitcast.23) | data formatting | bytes 829440
  31.5 0.0 copy-start.1
  31.5 0.0 copy-start.3
  31.5 0.0 copy-start.4
  31.5 0.6 pad.12.clone
  32.1 1.1 reshape.35.wg_ref
  33.2 0.0 copy-done
  33.2 0.5 copy.16
  33.7 0.4 reshape.36
  34.1 1.0 copy.20
  35.1 0.8 pad.13.clone
  35.9 0.0 copy-done.2
  35.9 0.1 reshape.30
  36.0 0.1 copy.22
  36.0 0.1 reshape.31
  36.2 0.1 copy.14
  36.3 0.0 copy-done.1
  36.3 0.2 reshape.32
  36.4 0.1 copy.13
  36.6 0.1 pad.18.clone
  36.7 0.1 pad.20.clone
  36.8 0.8 maximum_maximum_fusion.act_ref
  37.5 0.0 copy-done.3
  37.5 0.0 copy-done.4
  37.5 0.6 select_maximum_fusion.bias_ref
  38.1 279.1 %shard_map.64 = bf16[2,288,192]{2,1,0:T(8,128)(2,1)} custom-call(bf16[288,384]{1,0:T(8,128)(2,1)} %maximum_maximum_fusion.act_ref, bf16[9,64,384]{2,1,0:T(8,128)(2,1)} %reshape.35.wg_ref, bf16[9,64,192]{2,1,0:T(8,128)(2,1)} %bitcast.25, f32[8,256]{1,0:T(8,128)} %select_maximum_fusion.bias_ref), custom_call_target="tpu_custom_call" | custom-call | tf_op jit(solution)/shard_map/pallas_call | solution.py:392
  317.2 1.2 copy.18
  318.4 1.2 reshape.39
  (2 shorter events, 0.0 us)
Async XLA Ops:
  18.3 14.9 %copy-start = (bf16[30,3456]{1,0:T(8,128)(2,1)S(1)}, bf16[30,3456]{1,0:T(8,128)(2,1)}, u32[]{:S(2)}) copy-start(bf16[30,3456]{1,0:T(8,128)(2,1)} %param.10) | copy-start | bytes 622084
  18.3 17.5 %copy-start.2 = (bf16[2,3,4608]{2,0,1:T(2,128)(2,1)S(1)}, bf16[2,3,4608]{2,0,1:T(2,128)(2,1)}, u32[]{:S(2)}) copy-start(bf16[2,3,4608]{2,0,1:T(2,128)(2,1)} %param.7) | copy-start | bytes 165892
  31.5 4.8 %copy-start.1 = (bf16[3,18432]{1,0:T(4,128)(2,1)S(1)}, bf16[3,18432]{1,0:T(4,128)(2,1)}, u32[]{:S(2)}) copy-start(bf16[3,18432]{1,0:T(4,128)(2,1)} %param.6) | copy-start | bytes 331780
  31.5 6.0 %copy-start.3 = (f32[2,192]{1,0:T(2,128)S(1)}, f32[2,192]{1,0:T(2,128)}, u32[]{:S(2)}) copy-start(f32[2,192]{1,0:T(2,128)} %param.9) | copy-start | bytes 4612
  31.5 6.0 %copy-start.4 = (f32[192]{0:T(256)S(1)}, f32[192]{0:T(256)}, u32[]{:S(2)}) copy-start(f32[192]{0:T(256)} %param.11) | copy-start | bytes 2308

commit v2 on v1

--- a/solution.py
+++ b/solution.py
@@ -27,9 +27,8 @@
 
 
 def gate_taps(raw):
-    taps = raw.reshape(30, 2, OWN, 2, 9).transpose(4, 1, 0, 3, 2)
-    taps = jnp.pad(taps, ((0, 0), (0, 0), (0, 2), (0, 0), (0, 0)))
-    return taps.reshape(9, SLOT, 2 * OWN)
+    taps = raw.reshape(SHARD, OWN, 2, 3, 3).transpose(3, 4, 0, 2, 1).reshape(9, SHARD, 2 * OWN)
+    return jnp.pad(taps, ((0, 0), (0, SLOT - SHARD), (0, 0)))
 
 
 def cand_taps(raw):
@@ -41,7 +40,7 @@
 def kernel(
     act_ref, wg_ref, wc_ref, bias_ref, out_ref,
     init, gbuf0, sbuf, gbuf1, wg, wc, xs, emat, acc, cacc, upd, prev,
-    gated, fresh, landed, sib_bias,
+    fresh, landed, sib_bias,
     xsend, xrecv, wsend, wz, wl, wr, wo, wd, osem, orecv, bsem,
 ):
     s = lax.axis_index("space")
@@ -62,7 +61,7 @@
         )
 
     def greet_line(i, carry):
-        space, chan = 8 * x + i // 8, i % 8
+        space, chan = 8 * x + i // 2, 2 * y + i % 2
 
         @pl.when(jnp.logical_or(space != s, chan != ch))
         def _():
@@ -70,20 +69,25 @@
 
         return carry
 
-    lax.fori_loop(0, 64, greet_line, 0)
+    lax.fori_loop(0, 16, greet_line, 0)
     greet(8 * right + z, ch)
     greet(8 * left + z, ch)
-
-    @pl.when(z < 2)
+    up = 2 * ((y + 1) % 4) + c
+    down = 2 * ((y + 3) % 4) + c
+    greet(s, up)
+    greet(s, down)
+    first = jnp.logical_and(z < 2, c == 0)
+    last = jnp.logical_and(z >= 6, c == 1)
+
+    @pl.when(first)
     def _():
-        lax.fori_loop(0, 16, lambda i, k: (greet(8 * left + 6 + i // 8, i % 8), k)[1], 0)
-
-    @pl.when(z >= 6)
+        greet(8 * left + 6 + b, 2 * y + 1)
+
+    @pl.when(last)
     def _():
-        lax.fori_loop(0, 16, lambda i, k: (greet(8 * right + i // 8, i % 8), k)[1], 0)
-
-    at_end = jnp.logical_or(z < 2, z >= 6)
-    pl.semaphore_wait(barrier, 65 + 16 * at_end.astype(jnp.int32))
+        greet(8 * right + b, 2 * y)
+
+    pl.semaphore_wait(barrier, 19 + jnp.logical_or(first, last).astype(jnp.int32))
 
     def remote(src, dst, send, recv, space, chan):
         return pltpu.make_async_remote_copy(
@@ -112,39 +116,84 @@
     def arrived(dst, recv):
         pltpu.make_async_copy(dst, dst, recv).wait()
 
-    def exchange(act, k, row, chan, src, buf):
-        def one(i, carry):
-            kind, p = i // 8, i % 8
-            to_row = (row + jnp.where(kind == 0, 0, jnp.where(kind == 1, 1, 31))) % 32
-            space = to_row - to_row % 2 + p % 2
-            dest = p - p % 2 + to_row % 2
-
-            @pl.when(kind == 0)
-            def _():
-                act(src, buf.at[chan, pl.ds(W, CELLS)], xsend.at[i], xrecv.at[k, 0, chan], space, dest)
-
-            @pl.when(kind == 1)
-            def _():
-                act(src.at[pl.ds(2 * W, W)], buf.at[chan, pl.ds(0, W)], xsend.at[i],
-                    xrecv.at[k, 1, chan], space, dest)
-
-            @pl.when(kind == 2)
-            def _():
-                act(src.at[pl.ds(0, W)], buf.at[chan, pl.ds(4 * W, W)], xsend.at[i],
-                    xrecv.at[k, 2, chan], space, dest)
-
-            return carry
-
-        lax.fori_loop(0, 24, one, 0)
+    mate = s + 1 - 2 * b
+    half = HALO // 2
+    blocks = [2 * ((y + d) % 4) + b for d in (0, 3, 1, 2)]
+    twins = [2 * ((y + d) % 4) + 1 - b for d in (0, 3, 1, 2)]
+
+    def edge(k, buf, down_edge):
+        n = job_chan
+        to_row = (job_row + (1 if down_edge else 31)) % 32
+        src = buf.at[n, pl.ds(3 * W if down_edge else W, W)]
+        dst = buf.at[n, pl.ds(0 if down_edge else 4 * W, W)]
+        i = 0 if down_edge else 1
+        return remote(src, dst, xsend.at[i], xrecv.at[k, 16 + i],
+                      to_row - to_row % 2 + b, 2 * y + to_row % 2)
+
+    def part(buf, which, n):
+        return buf.at[n, pl.ds(which * half, half)]
+
+    def move(k, buf, which, n, i, space, chan):
+        ref = part(buf, which, n)
+        return remote(ref, ref, xsend.at[i], xrecv.at[k, 8 * which + n], space, chan)
+
+    def moves(k, buf):
+        own_a = [move(k, buf, 0, blocks[0], 2, s, up), move(k, buf, 0, blocks[0], 3, s, down)]
+        own_b = [move(k, buf, 1, blocks[0], 4, mate, ch),
+                 move(k, buf, 1, blocks[0], 5, s, up), move(k, buf, 1, blocks[0], 6, s, down)]
+        on_a = [move(k, buf, 0, blocks[d], 7 + d, mate, ch) for d in range(4)]
+        pass_a = move(k, buf, 0, blocks[1], 11, s, up)
+        mate_b = [move(k, buf, 1, twins[0], 12, s, up), move(k, buf, 1, twins[0], 13, s, down)]
+        pass_b = [move(k, buf, 1, blocks[2], 14, s, down), move(k, buf, 1, twins[2], 15, s, down)]
+        return own_a, own_b, on_a, pass_a, mate_b, pass_b
+
+    def got(k, buf, which, n):
+        arrived(part(buf, which, n), xrecv.at[k, 8 * which + n])
+
+    def edges_out(k, buf):
+        edge(k, buf, True).start()
+        edge(k, buf, False).start()
+
+    def exchange(k, buf):
+        own_a, own_b, on_a, pass_a, mate_b, pass_b = moves(k, buf)
+        arrived(buf.at[job_chan, pl.ds(0, W)], xrecv.at[k, 16])
+        for m in own_a:
+            m.start()
+        on_a[0].start()
+        arrived(buf.at[job_chan, pl.ds(4 * W, W)], xrecv.at[k, 17])
+        for m in own_b:
+            m.start()
+        got(k, buf, 0, blocks[1])
+        pass_a.start()
+        on_a[1].start()
+        got(k, buf, 0, blocks[2])
+        on_a[2].start()
+        got(k, buf, 1, twins[0])
+        for m in mate_b:
+            m.start()
+        got(k, buf, 1, blocks[2])
+        pass_b[0].start()
+        got(k, buf, 1, twins[2])
+        pass_b[1].start()
+        got(k, buf, 0, blocks[3])
+        on_a[3].start()
 
     def exchanged(k, buf):
-        def one(n, carry):
-            arrived(buf.at[n, pl.ds(W, CELLS)], xrecv.at[k, 0, n])
-            arrived(buf.at[n, pl.ds(0, W)], xrecv.at[k, 1, n])
-            arrived(buf.at[n, pl.ds(4 * W, W)], xrecv.at[k, 2, n])
-            return carry
-
-        lax.fori_loop(0, 8, one, 0)
+        for d in range(4):
+            got(k, buf, 0, twins[d])
+        for d in (1, 3):
+            got(k, buf, 1, blocks[d])
+            got(k, buf, 1, twins[d])
+
+    def exchange_sent(k, buf):
+        own_a, own_b, on_a, pass_a, mate_b, pass_b = moves(k, buf)
+        edge(k, buf, True).wait_send()
+        edge(k, buf, False).wait_send()
+        for m in own_a + own_b + on_a + [pass_a] + mate_b + pass_b:
+            m.wait_send()
+
+    def own_rows(buf):
+        return buf.at[job_chan, pl.ds(W, CELLS)]
 
     group = z // 4
     spot = z % 4
@@ -154,11 +203,16 @@
         src, buf = mine[kind]
 
         def one(i, carry):
+            to = (z // 2 + jnp.where(c == 0, i, 4 - i)) % 4
             act(src, buf.at[2 * x + group, :, spot], wsend.at[kind, i], wz.at[kind, spot],
-                8 * x + 2 * i + c, 2 * y + group)
+                8 * x + 2 * to + c, 2 * y + group)
             return carry
 
         lax.fori_loop(0, 4, one, 0)
+
+    lag = (z // 2 + 8 - 2 * c) % 4
+    head = jnp.where(b == 0, jnp.where(lag == 0, 0, 2), jnp.where(lag == 1, 2, 0))
+    turn = [(i + head) % 4 for i in range(4)]
 
     here, lower, upper, across = 2 * x + c, 2 * left + c, 2 * right + c, 2 * opposite + c
 
@@ -186,25 +240,25 @@
         return mine[kind][1].at[t, :, i]
 
     def kernel_own(kind):
-        for i in range(4):
+        for parity, i in zip((0, 1, 0, 1), turn):
             arrived(piece(kind, here, i), wz.at[kind, i])
             go_right(kind, i).start()
             go_left(kind, i).start()
             share(kind, 0, i).start()
 
     def kernel_sides(kind):
-        for i in range(4):
+        for parity, i in zip((0, 1, 0, 1), turn):
             arrived(piece(kind, lower, i), wl.at[kind, i])
-            if i % 2 == 0:
+            if parity == 0:
                 pass_right(kind, i).start()
             share(kind, 1, i).start()
             arrived(piece(kind, upper, i), wr.at[kind, i])
-            if i % 2 == 1:
+            if parity == 1:
                 pass_left(kind, i).start()
             share(kind, 2, i).start()
 
     def kernel_across(kind):
-        for i in range(4):
+        for parity, i in zip((0, 1, 0, 1), turn):
             arrived(piece(kind, across, i), wo.at[kind, i])
             share(kind, 3, i).start()
 
@@ -226,12 +280,14 @@
             for j in range(4):
                 share(kind, j, i).wait_send()
 
-    def slot_channel(t, rows):
+    def slot_channel(order, t, rows):
         j = lax.broadcasted_iota(jnp.int32, (rows, WIN), 1)
         r = j % SLOT
+        base = SHARD * (4 * t + j // SLOT)
+        if order == 0:
+            return jnp.where(r < SHARD, base + r, -1)
         m = r % 32
-        k = SHARD * (4 * t + j // SLOT) + 2 * m + r // 32
-        return jnp.where(m < 30, k, -1)
+        return jnp.where(m < 30, base + 2 * m + r // 32, -1)
 
     def spread(t, v):
         cell = lax.broadcasted_iota(jnp.int32, (HALO, WIN), 0)
@@ -247,10 +303,10 @@
         xs[:, 768 * t + 256:768 * t + 512] = v.astype(BF)
         xs[:, 768 * t + 512:768 * t + 768] = high.astype(BF)
 
-    def cond_slots(step, t):
+    def cond_slots(step, order, t):
         v = jnp.zeros((HALO, WIN), F32)
         lane = lax.broadcasted_iota(jnp.int32, (128, WIN), 0)
-        want = slot_channel(t, 128)
+        want = slot_channel(order, t, 128)
         for n in range(5 * t, min(8, 5 * t + 5)):
             here_n = jnp.logical_and(lane >= COND * step, lane < COND * step + COND)
             hit = jnp.logical_and(here_n, want == COND * n + lane - COND * step)
@@ -258,14 +314,13 @@
             v = v + jnp.dot(init[n, :, 0:128], e, preferred_element_type=F32)
         return v
 
-    def build(step, buf, base, first):
-        if first:
-            spread(0, cond_slots(step, 0))
+    def build(step, order, buf, base):
+        spread(0, cond_slots(step, order, 0))
         for t in range(1, 8):
-            v = cond_slots(step, 1) if t == 1 else jnp.zeros((HALO, WIN), F32)
+            v = cond_slots(step, order, 1) if t == 1 else jnp.zeros((HALO, WIN), F32)
             for q, (pt, n) in enumerate(PAIRS):
                 if pt == t:
-                    v = v + jnp.dot(buf[n, :, base:base + OWN], emat[q], preferred_element_type=F32)
+                    v = v + jnp.dot(buf[n, :, base:base + OWN], emat[order, q], preferred_element_type=F32)
             spread(t, v)
 
     def window(buf, total, t):
@@ -281,11 +336,11 @@
     def bias(row):
         return jnp.where(b == c, bias_ref[row:row + 1, 0:OWN], sib_bias[row:row + 1, 0:OWN])
 
-    def finish_gate(k):
+    def finish_gate(buf):
         pre = acc[...]
         upd[...] = jax.nn.sigmoid(pre[:, :OWN] + bias(0))
         reset = jax.nn.sigmoid(pltpu.roll(pre, OWN, 1)[:, :OWN] + bias(1))
-        gated[k] = (reset * prev[...]).astype(BF)
+        buf[job_chan, pl.ds(W, CELLS), :] = (reset * prev[...]).astype(BF)
 
     def finish_cand(k):
         candidate = jnp.tanh(cacc[...] + bias(2))
@@ -297,31 +352,35 @@
     def deliver(k, act):
         act(fresh.at[k], landed.at[k], osem.at[k], orecv.at[k], job_row, job_chan)
 
-    exchange(push, 0, s, ch, act_ref, init)
+    kernel_z(0, push)
+    first_copy = (act_ref, init.at[ch, pl.ds(W, CELLS)], bsem.at[2], bsem.at[3], job_row, job_chan)
+    push(*first_copy)
     bias_copy = remote(bias_ref, sib_bias, bsem.at[0], bsem.at[1], s, 2 * y + 1 - c)
     bias_copy.start()
-    kernel_z(0, push)
+    arrived(own_rows(init), bsem.at[3])
+    edges_out(0, init)
     kernel_z(1, push)
-    for q, (t, n) in enumerate(PAIRS):
-        lane = lax.broadcasted_iota(jnp.int32, (OWN, WIN), 0)
-        hit = slot_channel(t, OWN) == 384 + 192 * n + lane
-        emat[q] = hit.astype(F32).astype(BF)
+    for order in range(2):
+        for q, (t, n) in enumerate(PAIRS):
+            lane = lax.broadcasted_iota(jnp.int32, (OWN, WIN), 0)
+            hit = slot_channel(order, t, OWN) == 384 + 192 * n + lane
+            emat[order, q] = hit.astype(F32).astype(BF)
     acc[...] = jnp.zeros_like(acc)
     cacc[...] = jnp.zeros_like(cacc)
     kernel_own(0)
-    exchanged(0, init)
-    exchange(sent, 0, s, ch, act_ref, init)
-    bias_copy.wait()
-    prev[...] = init[job_chan, pl.ds(W, CELLS), 128:128 + OWN].astype(F32)
-    build(0, init, 128, True)
-
-    window(wg, acc, here)
+    exchange(0, init)
     kernel_sides(0)
     kernel_own(1)
+    sent(*first_copy)
+    bias_copy.wait()
+    exchanged(0, init)
+    prev[...] = init[job_chan, pl.ds(W, CELLS), 128:128 + OWN].astype(F32)
+    build(0, 0, init, 128)
 
     def shared_window(kind, buf, total, j):
         window(buf, total, kernel_shared(kind, j))
 
+    window(wg, acc, here)
     window(wg, acc, lower)
     window(wg, acc, upper)
     shared_window(0, wg, acc, 0)
@@ -330,12 +389,13 @@
     kernel_across(0)
     window(wg, acc, across)
     shared_window(0, wg, acc, 3)
-    finish_gate(0)
-    exchange(push, 1, job_row, job_chan, gated.at[0], gbuf0)
+    exchange_sent(0, init)
+    finish_gate(gbuf0)
+    edges_out(1, gbuf0)
+    exchange(1, gbuf0)
     kernel_sides(1)
     exchanged(1, gbuf0)
-    exchange(sent, 1, job_row, job_chan, gated.at[0], gbuf0)
-    build(0, gbuf0, 0, False)
+    build(0, 1, gbuf0, 0)
     window(wc, cacc, here)
     window(wc, cacc, lower)
     window(wc, cacc, upper)
@@ -345,15 +405,17 @@
     kernel_across(1)
     window(wc, cacc, across)
     shared_window(1, wc, cacc, 3)
+    exchange_sent(1, gbuf0)
     finish_cand(0)
 
-    exchange(push, 2, job_row, job_chan, fresh.at[0], sbuf)
+    sbuf[job_chan, pl.ds(W, CELLS), :] = fresh[0]
+    edges_out(2, sbuf)
     deliver(0, push)
     acc[...] = jnp.zeros_like(acc)
     cacc[...] = jnp.zeros_like(cacc)
+    exchange(2, sbuf)
     exchanged(2, sbuf)
-    exchange(sent, 2, job_row, job_chan, fresh.at[0], sbuf)
-    build(1, sbuf, 0, True)
+    build(1, 0, sbuf, 0)
 
     def all_windows(buf, total):
         def one(t, carry):
@@ -363,14 +425,16 @@
         lax.fori_loop(0, 8, one, 0)
 
     all_windows(wg, acc)
-    finish_gate(1)
-    exchange(push, 3, job_row, job_chan, gated.at[1], gbuf1)
+    exchange_sent(2, sbuf)
+    finish_gate(gbuf1)
+    edges_out(3, gbuf1)
+    exchange(3, gbuf1)
     kernel_sent(0)
     kernel_sent(1)
     exchanged(3, gbuf1)
-    exchange(sent, 3, job_row, job_chan, gated.at[1], gbuf1)
-    build(1, gbuf1, 0, False)
+    build(1, 1, gbuf1, 0)
     all_windows(wc, cacc)
+    exchange_sent(3, gbuf1)
     finish_cand(1)
     deliver(1, push)
     for k in range(2):
@@ -402,17 +466,16 @@
             pltpu.VMEM((8, 9, 4, SLOT, 2 * OWN), BF),
             pltpu.VMEM((8, 9, 4, SLOT, OWN), BF),
             pltpu.VMEM((HALO, 8 * 768), BF),
-            pltpu.VMEM((len(PAIRS), OWN, WIN), BF),
+            pltpu.VMEM((2, len(PAIRS), OWN, WIN), BF),
             pltpu.VMEM((CELLS, 2 * OWN), F32),
             pltpu.VMEM((CELLS, OWN), F32),
             pltpu.VMEM((CELLS, OWN), F32),
             pltpu.VMEM((CELLS, OWN), F32),
             pltpu.VMEM((2, CELLS, OWN), BF),
             pltpu.VMEM((2, CELLS, OWN), BF),
-            pltpu.VMEM((2, CELLS, OWN), BF),
             pltpu.VMEM((8, 256), F32),
-            dma((24,)),
-            dma((4, 3, 8)),
+            dma((16,)),
+            dma((4, 18)),
             dma((2, 32)),
             dma((2, 4)),
             dma((2, 4)),
@@ -421,7 +484,7 @@
             dma((2, 4, 4)),
             dma((2,)),
             dma((2,)),
-            dma((2,)),
+            dma((4,)),
         ],
         compiler_params=pltpu.CompilerParams(
             collective_id=0, has_side_effects=True, vmem_limit_bytes=63 * 1024 * 1024

time: 320 us -> 232 us (0.72); the launches traced: 320 us -> 228 us
  Pallas kernels: 279 us -> 216 us
  local copies, waits for them, and re-layouts: 39 us -> 10.2 us
    pallas_call x1, Pallas kernels: 279 us -> 216 us  [local(): pl.pallas_call(kernel, out_shape=jax.ShapeDtypeStruct((2, CELLS, OWN), BF...]
    reshape x2, local copies, waits for them, and re-layouts: 19.4 us -> 0.92 us  [gate_taps(): raw.reshape(SHARD, OWN, 2, 3, 3).transpose(3, 4, 0, 2, 1)]
    unnamed x13, local copies, waits for them, and re-layouts: 14.7 us -> 2.93 us
where the time goes in v2:
time: 232 us; the launch traced here: 228 us
  Pallas kernels  216 us (93%)
  local copies, waits for them, and re-layouts  10.2 us (4%)
    pallas_call x1, Pallas kernels, local(): pl.pallas_call(kernel, out_shape=jax.ShapeDtypeStruct((2, CELLS, OWN), BF...  216 us

profile of v2, /device:TPU:31, one launch (start us, length us, event | category | flops | bytes accessed | tf_op | source)
XLA Modules:
  0.0 228.2 jit_solution(12093656237089930609)
XLA Ops:
  0.0 1.5 copy.15
  1.5 0.6 reshape.34
  2.0 0.0 copy-start
  2.1 1.2 copy.16
  3.3 0.3 reshape.35
  3.6 0.8 pad.12.wg_ref
  4.4 0.0 copy-done
  4.4 0.5 copy.17
  4.9 0.4 reshape.36
  5.3 0.0 copy-start.2
  5.3 0.0 copy-start.1
  5.3 1.0 copy.20
  6.3 0.0 copy-start.3
  6.3 0.0 copy-start.4
  6.4 0.8 pad.13.clone
  7.1 0.0 copy-done.2
  7.1 0.1 reshape.30
  7.2 0.1 copy.22
  7.3 0.1 reshape.31
  7.4 0.1 copy.14
  7.5 0.0 copy-done.1
  7.6 0.2 reshape.32
  7.7 0.1 copy.13
  7.9 0.1 pad.18.clone
  8.0 0.1 pad.20.clone
  8.0 0.8 maximum_maximum_fusion.act_ref
  8.8 0.0 copy-done.3
  8.8 0.0 copy-done.4
  8.8 0.6 select_maximum_fusion.bias_ref
  9.4 216.5 %shard_map.64 = bf16[2,288,192]{2,1,0:T(8,128)(2,1)} custom-call(bf16[288,384]{1,0:T(8,128)(2,1)} %maximum_maximum_fusion.act_ref, bf16[9,64,384]{2,1,0:T(8,128)(2,1)} %pad.12.wg_ref, bf16[9,64,192]{2,1,0:T(8,128)(2,1)} %bitcast.27, f32[8,256]{1,0:T(8,128)} %select_maximum_fusion.bias_ref), custom_call_target="tpu_custom_call" | custom-call | tf_op jit(solution)/shard_map/pallas_call | solution.py:456
  225.9 1.2 copy.19
  227.1 1.2 reshape.39
  (2 shorter events, 0.0 us)
Async XLA Ops:
  2.0 2.4 %copy-start = (bf16[30,3456]{1,0:T(8,128)(2,1)S(1)}, bf16[30,3456]{1,0:T(8,128)(2,1)}, u32[]{:S(2)}) copy-start(bf16[30,3456]{1,0:T(8,128)(2,1)} %param.10) | copy-start | bytes 622084
  5.3 1.8 copy-start.2
  5.3 2.2 copy-start.1
  6.3 2.5 %copy-start.3 = (f32[2,192]{1,0:T(2,128)S(1)}, f32[2,192]{1,0:T(2,128)}, u32[]{:S(2)}) copy-start(f32[2,192]{1,0:T(2,128)} %param.9) | copy-start | bytes 4612
  6.3 2.4 %copy-start.4 = (f32[192]{0:T(256)S(1)}, f32[192]{0:T(256)}, u32[]{:S(2)}) copy-start(f32[192]{0:T(256)} %param.11) | copy-start | bytes 2308

commit v3 on v2

--- a/solution.py
+++ b/solution.py
@@ -34,7 +34,7 @@
 def cand_taps(raw):
     taps = raw.reshape(30, OWN, 2, 9).transpose(3, 2, 0, 1)
     taps = jnp.pad(taps, ((0, 0), (0, 0), (0, 2), (0, 0)))
-    return taps.reshape(9, SLOT, OWN)
+    return jnp.concatenate([taps[:, 0], taps[:, 1]], axis=2)
 
 
 def kernel(
@@ -117,7 +117,7 @@
         pltpu.make_async_copy(dst, dst, recv).wait()
 
     mate = s + 1 - 2 * b
-    half = HALO // 2
+    spans = ((W, CELLS // 2), (W + CELLS // 2, CELLS // 2), (0, W), (4 * W, W))
     blocks = [2 * ((y + d) % 4) + b for d in (0, 3, 1, 2)]
     twins = [2 * ((y + d) % 4) + 1 - b for d in (0, 3, 1, 2)]
 
@@ -127,24 +127,26 @@
         src = buf.at[n, pl.ds(3 * W if down_edge else W, W)]
         dst = buf.at[n, pl.ds(0 if down_edge else 4 * W, W)]
         i = 0 if down_edge else 1
-        return remote(src, dst, xsend.at[i], xrecv.at[k, 16 + i],
+        return remote(src, dst, xsend.at[i], xrecv.at[k, 32 + i],
                       to_row - to_row % 2 + b, 2 * y + to_row % 2)
 
     def part(buf, which, n):
-        return buf.at[n, pl.ds(which * half, half)]
+        return buf.at[n, pl.ds(*spans[which])]
 
     def move(k, buf, which, n, i, space, chan):
         ref = part(buf, which, n)
-        return remote(ref, ref, xsend.at[i], xrecv.at[k, 8 * which + n], space, chan)
-
-    def moves(k, buf):
-        own_a = [move(k, buf, 0, blocks[0], 2, s, up), move(k, buf, 0, blocks[0], 3, s, down)]
-        own_b = [move(k, buf, 1, blocks[0], 4, mate, ch),
-                 move(k, buf, 1, blocks[0], 5, s, up), move(k, buf, 1, blocks[0], 6, s, down)]
-        on_a = [move(k, buf, 0, blocks[d], 7 + d, mate, ch) for d in range(4)]
-        pass_a = move(k, buf, 0, blocks[1], 11, s, up)
-        mate_b = [move(k, buf, 1, twins[0], 12, s, up), move(k, buf, 1, twins[0], 13, s, down)]
-        pass_b = [move(k, buf, 1, blocks[2], 14, s, down), move(k, buf, 1, twins[2], 15, s, down)]
+        send = xsend.at[2 + 14 * (which // 2) + i]
+        return remote(ref, ref, send, xrecv.at[k, 8 * which + n], space, chan)
+
+    def moves(k, buf, g):
+        p, q = 2 * g, 2 * g + 1
+        own_a = [move(k, buf, p, blocks[0], 0, s, up), move(k, buf, p, blocks[0], 1, s, down)]
+        own_b = [move(k, buf, q, blocks[0], 2, mate, ch),
+                 move(k, buf, q, blocks[0], 3, s, up), move(k, buf, q, blocks[0], 4, s, down)]
+        on_a = [move(k, buf, p, blocks[d], 5 + d, mate, ch) for d in range(4)]
+        pass_a = move(k, buf, p, blocks[1], 9, s, up)
+        mate_b = [move(k, buf, q, twins[0], 10, s, up), move(k, buf, q, twins[0], 11, s, down)]
+        pass_b = [move(k, buf, q, blocks[2], 12, s, down), move(k, buf, q, twins[2], 13, s, down)]
         return own_a, own_b, on_a, pass_a, mate_b, pass_b
 
     def got(k, buf, which, n):
@@ -154,43 +156,57 @@
         edge(k, buf, True).start()
         edge(k, buf, False).start()
 
-    def exchange(k, buf):
-        own_a, own_b, on_a, pass_a, mate_b, pass_b = moves(k, buf)
-        arrived(buf.at[job_chan, pl.ds(0, W)], xrecv.at[k, 16])
-        for m in own_a:
+    def exchange_own(k, buf, g):
+        own_a, own_b, on_a, _, _, _ = moves(k, buf, g)
+        if g == 1:
+            arrived(part(buf, 2, job_chan), xrecv.at[k, 32])
+            arrived(part(buf, 3, job_chan), xrecv.at[k, 33])
+        for m in [own_b[0]] + own_a + [on_a[0]] + own_b[1:]:
             m.start()
-        on_a[0].start()
-        arrived(buf.at[job_chan, pl.ds(4 * W, W)], xrecv.at[k, 17])
-        for m in own_b:
+
+    def exchange_on(k, buf, g):
+        _, _, on_a, pass_a, mate_b, pass_b = moves(k, buf, g)
+        p, q = 2 * g, 2 * g + 1
+        got(k, buf, q, twins[0])
+        for m in mate_b:
             m.start()
-        got(k, buf, 0, blocks[1])
+        got(k, buf, p, blocks[1])
         pass_a.start()
         on_a[1].start()
-        got(k, buf, 0, blocks[2])
+        got(k, buf, p, blocks[2])
         on_a[2].start()
-        got(k, buf, 1, twins[0])
-        for m in mate_b:
-            m.start()
-        got(k, buf, 1, blocks[2])
+        got(k, buf, q, blocks[2])
         pass_b[0].start()
-        got(k, buf, 1, twins[2])
+        got(k, buf, q, twins[2])
         pass_b[1].start()
-        got(k, buf, 0, blocks[3])
-        on_a[3].start()
+
+    def exchange(k, buf):
+        exchange_own(k, buf, 0)
+        exchange_own(k, buf, 1)
+        exchange_rest(k, buf)
+
+    def exchange_rest(k, buf):
+        exchange_on(k, buf, 0)
+        exchange_on(k, buf, 1)
+        for g in range(2):
+            got(k, buf, 2 * g, blocks[3])
+            moves(k, buf, g)[2][3].start()
 
     def exchanged(k, buf):
-        for d in range(4):
-            got(k, buf, 0, twins[d])
-        for d in (1, 3):
-            got(k, buf, 1, blocks[d])
-            got(k, buf, 1, twins[d])
+        for g in range(2):
+            for d in range(4):
+                got(k, buf, 2 * g, twins[d])
+            for d in (1, 3):
+                got(k, buf, 2 * g + 1, blocks[d])
+                got(k, buf, 2 * g + 1, twins[d])
 
     def exchange_sent(k, buf):
-        own_a, own_b, on_a, pass_a, mate_b, pass_b = moves(k, buf)
         edge(k, buf, True).wait_send()
         edge(k, buf, False).wait_send()
-        for m in own_a + own_b + on_a + [pass_a] + mate_b + pass_b:
-            m.wait_send()
+        for g in range(2):
+            own_a, own_b, on_a, pass_a, mate_b, pass_b = moves(k, buf, g)
+            for m in own_a + own_b + on_a + [pass_a] + mate_b + pass_b:
+                m.wait_send()
 
     def own_rows(buf):
         return buf.at[job_chan, pl.ds(W, CELLS)]
@@ -199,16 +215,11 @@
     spot = z % 4
     mine = ((wg_ref, wg), (wc_ref, wc))
 
-    def kernel_z(kind, act):
+    def kernel_z(kind, act, i):
         src, buf = mine[kind]
-
-        def one(i, carry):
-            to = (z // 2 + jnp.where(c == 0, i, 4 - i)) % 4
-            act(src, buf.at[2 * x + group, :, spot], wsend.at[kind, i], wz.at[kind, spot],
-                8 * x + 2 * to + c, 2 * y + group)
-            return carry
-
-        lax.fori_loop(0, 4, one, 0)
+        to = (z // 2 + (0 if i == 0 else jnp.where(c == 0, i, 4 - i))) % 4
+        act(src, buf.at[2 * x + group, :, spot], wsend.at[kind, i], wz.at[kind, spot],
+            8 * x + 2 * to + c, 2 * y + group)
 
     lag = (z // 2 + 8 - 2 * c) % 4
     head = jnp.where(b == 0, jnp.where(lag == 0, 0, 2), jnp.where(lag == 1, 2, 0))
@@ -239,15 +250,40 @@
     def piece(kind, t, i):
         return mine[kind][1].at[t, :, i]
 
-    def kernel_own(kind):
+    def onward(kind, parity, i):
+        return hop(kind, here, i, 2 if parity == 0 else 32, wz.at[kind, i],
+                   8 * x + (z + jnp.where(b == 0, 2, 6)) % 8, ch)
+
+    def passes_on(i):
+        source = 2 * c + i // 2
+        steps = jnp.where(b == 0, z // 2 - source + 4, source - z // 2 + 4) % 4
+        return steps == 1
+
+    def kernel_relay(kind):
         for parity, i in zip((0, 1, 0, 1), turn):
-            arrived(piece(kind, here, i), wz.at[kind, i])
+            @pl.when(passes_on(i))
+            def _():
+                arrived(piece(kind, here, i), wz.at[kind, i])
+                onward(kind, parity, i).start()
+
+    def kernel_own(kind, relayed, pair):
+        for parity, i in zip((0, 1), turn[2 * pair:2 * pair + 2]):
+            if relayed:
+                @pl.when(jnp.logical_not(passes_on(i)))
+                def _():
+                    arrived(piece(kind, here, i), wz.at[kind, i])
+            else:
+                arrived(piece(kind, here, i), wz.at[kind, i])
+
+                @pl.when(passes_on(i))
+                def _():
+                    onward(kind, parity, i).start()
             go_right(kind, i).start()
             go_left(kind, i).start()
             share(kind, 0, i).start()
 
-    def kernel_sides(kind):
-        for parity, i in zip((0, 1, 0, 1), turn):
+    def kernel_sides(kind, pair):
+        for parity, i in zip((0, 1), turn[2 * pair:2 * pair + 2]):
             arrived(piece(kind, lower, i), wl.at[kind, i])
             if parity == 0:
                 pass_right(kind, i).start()
@@ -269,7 +305,12 @@
         return t
 
     def kernel_sent(kind):
-        kernel_z(kind, sent)
+        for i in (0, 3) if kind == 0 else (0, 1, 3):
+            kernel_z(kind, sent, i)
+        for parity, i in zip((0, 1, 0, 1), turn):
+            @pl.when(passes_on(i))
+            def _():
+                onward(kind, parity, i).wait_send()
         for i in range(4):
             go_right(kind, i).wait_send()
             go_left(kind, i).wait_send()
@@ -282,14 +323,13 @@
 
     def slot_channel(order, t, rows):
         j = lax.broadcasted_iota(jnp.int32, (rows, WIN), 1)
-        r = j % SLOT
-        base = SHARD * (4 * t + j // SLOT)
         if order == 0:
-            return jnp.where(r < SHARD, base + r, -1)
-        m = r % 32
-        return jnp.where(m < 30, base + 2 * m + r // 32, -1)
-
-    def spread(t, v):
+            r = j % SLOT
+            return jnp.where(r < SHARD, SHARD * (4 * t + j // SLOT) + r, -1)
+        m = j % 32
+        return jnp.where(m < 30, SHARD * (4 * t + j % 128 // 32) + 2 * m + j // 128, -1)
+
+    def spread(order, t, v):
         cell = lax.broadcasted_iota(jnp.int32, (HALO, WIN), 0)
         col = cell % W
         inside = jnp.logical_and(
@@ -299,9 +339,14 @@
         v = jnp.where(inside, v, 0.0)
         low = jnp.where(col == 0, 0.0, pltpu.roll(v, 1, 0))
         high = jnp.where(col == W - 1, 0.0, pltpu.roll(v, HALO - 1, 0))
-        xs[:, 768 * t:768 * t + 256] = low.astype(BF)
-        xs[:, 768 * t + 256:768 * t + 512] = v.astype(BF)
-        xs[:, 768 * t + 512:768 * t + 768] = high.astype(BF)
+        for d, shifted in enumerate((low, v, high)):
+            shifted = shifted.astype(BF)
+            if order == 0:
+                xs[:, 768 * t + 256 * d:768 * t + 256 * d + 256] = shifted
+            else:
+                for p in range(2):
+                    at = 768 * t + 384 * p + 128 * d
+                    xs[:, at:at + 128] = shifted[:, 128 * p:128 * p + 128]
 
     def cond_slots(step, order, t):
         v = jnp.zeros((HALO, WIN), F32)
@@ -315,23 +360,25 @@
         return v
 
     def build(step, order, buf, base):
-        spread(0, cond_slots(step, order, 0))
+        spread(order, 0, cond_slots(step, order, 0))
         for t in range(1, 8):
             v = cond_slots(step, order, 1) if t == 1 else jnp.zeros((HALO, WIN), F32)
             for q, (pt, n) in enumerate(PAIRS):
                 if pt == t:
                     v = v + jnp.dot(buf[n, :, base:base + OWN], emat[order, q], preferred_element_type=F32)
-            spread(t, v)
+            spread(order, t, v)
 
     def window(buf, total, t):
-        lane = pl.multiple_of(768 * t, 768)
-        out = total.shape[1]
-        for a in range(3):
-            total[...] += jnp.dot(
-                xs[pl.ds(a * W, CELLS), pl.ds(lane, 768)],
-                buf[t, 3 * a:3 * a + 3].reshape(768, out),
-                preferred_element_type=F32,
-            )
+        depth = 2 * OWN if total is cacc else 768
+        for p in range(768 // depth):
+            lane = pl.multiple_of(768 * t + depth * p, depth)
+            sums = total.at[p] if total is cacc else total
+            for a in range(3):
+                sums[...] += jnp.dot(
+                    xs[pl.ds(a * W, CELLS), pl.ds(lane, depth)],
+                    buf[t, 3 * a:3 * a + 3].reshape(depth, 2 * OWN),
+                    preferred_element_type=F32,
+                )
 
     def bias(row):
         return jnp.where(b == c, bias_ref[row:row + 1, 0:OWN], sib_bias[row:row + 1, 0:OWN])
@@ -343,7 +390,7 @@
         buf[job_chan, pl.ds(W, CELLS), :] = (reset * prev[...]).astype(BF)
 
     def finish_cand(k):
-        candidate = jnp.tanh(cacc[...] + bias(2))
+        candidate = jnp.tanh(cacc[0][:, :OWN] + pltpu.roll(cacc[1], OWN, 1)[:, :OWN] + bias(2))
         u = upd[...]
         new = ((1.0 - u) * prev[...] + u * candidate).astype(BF)
         fresh[k] = new
@@ -352,14 +399,28 @@
     def deliver(k, act):
         act(fresh.at[k], landed.at[k], osem.at[k], orecv.at[k], job_row, job_chan)
 
-    kernel_z(0, push)
+    def kernel_z_rest():
+        kernel_z(0, sent, 1)
+        kernel_z(0, push, 3)
+
+    kernel_z(0, push, 0)
+    kernel_z(0, push, 1)
     first_copy = (act_ref, init.at[ch, pl.ds(W, CELLS)], bsem.at[2], bsem.at[3], job_row, job_chan)
     push(*first_copy)
     bias_copy = remote(bias_ref, sib_bias, bsem.at[0], bsem.at[1], s, 2 * y + 1 - c)
     bias_copy.start()
+    late = jnp.where(b == 0, lag, (4 - lag) % 4) == jnp.where(b == 0, 3, 2)
+    pl.when(late)(kernel_z_rest)
+    kernel_own(0, False, 0)
+    pl.when(jnp.logical_not(late))(kernel_z_rest)
     arrived(own_rows(init), bsem.at[3])
     edges_out(0, init)
-    kernel_z(1, push)
+    kernel_own(0, False, 1)
+    for i in (0, 1, 3):
+        kernel_z(1, push, i)
+    exchange_own(0, init, 0)
+    exchange_own(0, init, 1)
+    kernel_sides(0, 0)
     for order in range(2):
         for q, (t, n) in enumerate(PAIRS):
             lane = lax.broadcasted_iota(jnp.int32, (OWN, WIN), 0)
@@ -367,10 +428,11 @@
             emat[order, q] = hit.astype(F32).astype(BF)
     acc[...] = jnp.zeros_like(acc)
     cacc[...] = jnp.zeros_like(cacc)
-    kernel_own(0)
-    exchange(0, init)
-    kernel_sides(0)
-    kernel_own(1)
+    exchange_rest(0, init)
+    kernel_relay(1)
+    kernel_sides(0, 1)
+    kernel_own(1, True, 0)
+    kernel_own(1, True, 1)
     sent(*first_copy)
     bias_copy.wait()
     exchanged(0, init)
@@ -393,7 +455,8 @@
     finish_gate(gbuf0)
     edges_out(1, gbuf0)
     exchange(1, gbuf0)
-    kernel_sides(1)
+    kernel_sides(1, 0)
+    kernel_sides(1, 1)
     exchanged(1, gbuf0)
     build(0, 1, gbuf0, 0)
     window(wc, cacc, here)
@@ -464,19 +527,19 @@
             pltpu.VMEM((8, HALO, OWN), BF),
             pltpu.VMEM((8, HALO, OWN), BF),
             pltpu.VMEM((8, 9, 4, SLOT, 2 * OWN), BF),
-            pltpu.VMEM((8, 9, 4, SLOT, OWN), BF),
+            pltpu.VMEM((8, 9, 4, SLOT // 2, 2 * OWN), BF),
             pltpu.VMEM((HALO, 8 * 768), BF),
             pltpu.VMEM((2, len(PAIRS), OWN, WIN), BF),
             pltpu.VMEM((CELLS, 2 * OWN), F32),
-            pltpu.VMEM((CELLS, OWN), F32),
+            pltpu.VMEM((2, CELLS, 2 * OWN), F32),
             pltpu.VMEM((CELLS, OWN), F32),
             pltpu.VMEM((CELLS, OWN), F32),
             pltpu.VMEM((2, CELLS, OWN), BF),
             pltpu.VMEM((2, CELLS, OWN), BF),
             pltpu.VMEM((8, 256), F32),
-            dma((16,)),
-            dma((4, 18)),
-            dma((2, 32)),
+            dma((30,)),
+            dma((4, 34)),
+            dma((2, 33)),
             dma((2, 4)),
             dma((2, 4)),
             dma((2, 4)),

time: 232 us -> 206 us (0.89)
  Pallas kernels: 216 us -> 191 us
    pallas_call x1, Pallas kernels: 216 us -> 191 us  [local(): pl.pallas_call(kernel, out_shape=jax.ShapeDtypeStruct((2, CELLS, OWN), BF...]
where the time goes in v3:
time: 206 us; the launch traced here: 203 us
  Pallas kernels  191 us (93%)
  local copies, waits for them, and re-layouts  9.43 us (5%)
  other arithmetic  2.17 us (1%)
    pallas_call x1, Pallas kernels, local(): pl.pallas_call(kernel, out_shape=jax.ShapeDtypeStruct((2, CELLS, OWN), BF...  191 us

profile of v3, /device:TPU:31, one launch (start us, length us, event | category | flops | bytes accessed | tf_op | source)
XLA Modules:
  0.0 202.7 jit_solution(6890501590718560867)
XLA Ops:
  0.0 1.4 copy.16
  1.4 0.4 reshape.33
  1.8 0.0 copy-start
  1.8 1.0 copy.17
  2.8 0.1 fusion
  2.9 0.8 pad_maximum_fusion.wc_ref
  3.7 0.0 copy-done
  3.7 0.4 copy.14
  4.1 0.6 reshape.31
  4.7 0.0 copy-start.2
  4.7 1.2 copy.15
  6.0 0.0 copy-start.1
  6.0 0.0 copy-start.3
  6.0 0.0 copy-start.4
  6.0 0.3 reshape.32
  6.3 0.8 pad.12.wg_ref
  7.2 0.0 copy-done.2
  7.2 0.1 reshape.27
  7.3 0.1 copy.20
  7.3 0.1 reshape.28
  7.5 0.1 copy.13
  7.6 0.0 copy-done.1
  7.6 0.2 reshape.29
  7.7 0.1 copy.12
  7.9 0.1 pad.20.clone
  8.0 0.1 pad.22.clone
  8.1 0.8 maximum_maximum_fusion.act_ref
  8.8 0.0 copy-done.3
  8.8 0.6 select_maximum_fusion.bias_ref
  9.4 191.0 %shard_map.64 = bf16[2,288,192]{2,1,0:T(8,128)(2,1)} custom-call(bf16[288,384]{1,0:T(8,128)(2,1)} %maximum_maximum_fusion.act_ref, bf16[9,64,384]{2,1,0:T(8,128)(2,1)} %pad.12.wg_ref, bf16[9,32,384]{2,1,0:T(8,128)(2,1)} %pad_maximum_fusion.wc_ref, f32[8,256]{1,0:T(8,128)} %select_maximum_fusion.bias_ref), custom_call_target="tpu_custom_call" | custom-call | tf_op jit(solution)/shard_map/pallas_call | solution.py:519
  200.4 1.2 copy.18
  201.5 1.2 reshape.35
  (3 shorter events, 0.0 us)
Async XLA Ops:
  1.8 1.9 copy-start
  4.7 2.4 %copy-start.2 = (bf16[2,3,4608]{2,0,1:T(2,128)(2,1)S(1)}, bf16[2,3,4608]{2,0,1:T(2,128)(2,1)}, u32[]{:S(2)}) copy-start(bf16[2,3,4608]{2,0,1:T(2,128)(2,1)} %param.7) | copy-start | bytes 165892
  6.0 1.6 copy-start.1
  6.0 2.9 %copy-start.3 = (f32[2,192]{1,0:T(2,128)S(1)}, f32[2,192]{1,0:T(2,128)}, u32[]{:S(2)}) copy-start(f32[2,192]{1,0:T(2,128)} %param.9) | copy-start | bytes 4612
  6.0 2.8 %copy-start.4 = (f32[192]{0:T(256)S(1)}, f32[192]{0:T(256)}, u32[]{:S(2)}) copy-start(f32[192]{0:T(256)} %param.11) | copy-start | bytes 2308

commit v4 on v3

--- a/solution.py
+++ b/solution.py
@@ -117,21 +117,25 @@
         pltpu.make_async_copy(dst, dst, recv).wait()
 
     mate = s + 1 - 2 * b
-    spans = ((W, CELLS // 2), (W + CELLS // 2, CELLS // 2), (0, W), (4 * W, W))
+    spans = {
+        HALO: ((W, CELLS // 2), (W + CELLS // 2, CELLS // 2), (0, W), (4 * W, W)),
+        HALO // 2: ((48, 80), (128, 64), (0, 48), (192, 48)),
+    }
     blocks = [2 * ((y + d) % 4) + b for d in (0, 3, 1, 2)]
     twins = [2 * ((y + d) % 4) + 1 - b for d in (0, 3, 1, 2)]
 
     def edge(k, buf, down_edge):
         n = job_chan
         to_row = (job_row + (1 if down_edge else 31)) % 32
-        src = buf.at[n, pl.ds(3 * W if down_edge else W, W)]
-        dst = buf.at[n, pl.ds(0 if down_edge else 4 * W, W)]
+        unit = buf.shape[1] // 5
+        src = buf.at[n, pl.ds(3 * unit if down_edge else unit, unit)]
+        dst = buf.at[n, pl.ds(0 if down_edge else 4 * unit, unit)]
         i = 0 if down_edge else 1
         return remote(src, dst, xsend.at[i], xrecv.at[k, 32 + i],
                       to_row - to_row % 2 + b, 2 * y + to_row % 2)
 
     def part(buf, which, n):
-        return buf.at[n, pl.ds(*spans[which])]
+        return buf.at[n, pl.ds(*spans[buf.shape[1]][which])]
 
     def move(k, buf, which, n, i, space, chan):
         ref = part(buf, which, n)
@@ -185,8 +189,9 @@
         exchange_own(k, buf, 1)
         exchange_rest(k, buf)
 
-    def exchange_rest(k, buf):
+    def exchange_rest(k, buf, between=lambda: None):
         exchange_on(k, buf, 0)
+        between()
         exchange_on(k, buf, 1)
         for g in range(2):
             got(k, buf, 2 * g, blocks[3])
@@ -360,12 +365,18 @@
         return v
 
     def build(step, order, buf, base):
-        spread(order, 0, cond_slots(step, order, 0))
         for t in range(1, 8):
             v = cond_slots(step, order, 1) if t == 1 else jnp.zeros((HALO, WIN), F32)
             for q, (pt, n) in enumerate(PAIRS):
                 if pt == t:
-                    v = v + jnp.dot(buf[n, :, base:base + OWN], emat[order, q], preferred_element_type=F32)
+                    e = emat[order, q]
+                    low = jnp.dot(buf[n, :, base:base + OWN], e[64:], preferred_element_type=F32)
+                    if buf.shape[1] < HALO:
+                        high = jnp.dot(buf[n, :, 128:384], e, preferred_element_type=F32)
+                        low = jnp.concatenate(
+                            [low.reshape(5, 48, WIN), high.reshape(5, 48, WIN)], axis=1
+                        ).reshape(HALO, WIN)
+                    v = v + low
             spread(order, t, v)
 
     def window(buf, total, t):
@@ -383,11 +394,20 @@
     def bias(row):
         return jnp.where(b == c, bias_ref[row:row + 1, 0:OWN], sib_bias[row:row + 1, 0:OWN])
 
+    def pack(v, buf):
+        acc[:, 0:OWN] = v
+        flat = acc[...]
+        moved = pltpu.roll(flat, OWN, 1)
+        lane = lax.broadcasted_iota(jnp.int32, (48, 2 * OWN), 1)
+        for r in range(ROWS):
+            both = jnp.where(lane < OWN, flat[W * r:W * r + 48], moved[W * r + 48:W * r + W])
+            buf[job_chan, pl.ds(48 + 48 * r, 48), :] = both.astype(BF)
+
     def finish_gate(buf):
         pre = acc[...]
         upd[...] = jax.nn.sigmoid(pre[:, :OWN] + bias(0))
         reset = jax.nn.sigmoid(pltpu.roll(pre, OWN, 1)[:, :OWN] + bias(1))
-        buf[job_chan, pl.ds(W, CELLS), :] = (reset * prev[...]).astype(BF)
+        pack(reset * prev[...], buf)
 
     def finish_cand(k):
         candidate = jnp.tanh(cacc[0][:, :OWN] + pltpu.roll(cacc[1], OWN, 1)[:, :OWN] + bias(2))
@@ -423,8 +443,9 @@
     kernel_sides(0, 0)
     for order in range(2):
         for q, (t, n) in enumerate(PAIRS):
-            lane = lax.broadcasted_iota(jnp.int32, (OWN, WIN), 0)
-            hit = slot_channel(order, t, OWN) == 384 + 192 * n + lane
+            lane = lax.broadcasted_iota(jnp.int32, (256, WIN), 0)
+            hit = slot_channel(order, t, 256) == 320 + 192 * n + lane
+            hit = jnp.logical_and(hit, lane >= 64)
             emat[order, q] = hit.astype(F32).astype(BF)
     acc[...] = jnp.zeros_like(acc)
     cacc[...] = jnp.zeros_like(cacc)
@@ -437,6 +458,7 @@
     bias_copy.wait()
     exchanged(0, init)
     prev[...] = init[job_chan, pl.ds(W, CELLS), 128:128 + OWN].astype(F32)
+    spread(0, 0, cond_slots(0, 0, 0))
     build(0, 0, init, 128)
 
     def shared_window(kind, buf, total, j):
@@ -454,9 +476,11 @@
     exchange_sent(0, init)
     finish_gate(gbuf0)
     edges_out(1, gbuf0)
-    exchange(1, gbuf0)
+    exchange_own(1, gbuf0, 0)
+    exchange_own(1, gbuf0, 1)
     kernel_sides(1, 0)
-    kernel_sides(1, 1)
+    exchange_rest(1, gbuf0, lambda: kernel_sides(1, 1))
+    spread(1, 0, cond_slots(0, 1, 0))
     exchanged(1, gbuf0)
     build(0, 1, gbuf0, 0)
     window(wc, cacc, here)
@@ -471,12 +495,14 @@
     exchange_sent(1, gbuf0)
     finish_cand(0)
 
-    sbuf[job_chan, pl.ds(W, CELLS), :] = fresh[0]
+    pack(prev[...], sbuf)
     edges_out(2, sbuf)
     deliver(0, push)
     acc[...] = jnp.zeros_like(acc)
     cacc[...] = jnp.zeros_like(cacc)
     exchange(2, sbuf)
+    spread(0, 0, cond_slots(1, 0, 0))
+    window(wg, acc, 0)
     exchanged(2, sbuf)
     build(1, 0, sbuf, 0)
 
@@ -485,13 +511,15 @@
             window(buf, total, t)
             return carry
 
-        lax.fori_loop(0, 8, one, 0)
+        lax.fori_loop(1, 8, one, 0)
 
     all_windows(wg, acc)
     exchange_sent(2, sbuf)
     finish_gate(gbuf1)
     edges_out(3, gbuf1)
     exchange(3, gbuf1)
+    spread(1, 0, cond_slots(1, 1, 0))
+    window(wc, cacc, 0)
     kernel_sent(0)
     kernel_sent(1)
     exchanged(3, gbuf1)
@@ -523,13 +551,13 @@
         out_specs=vmem,
         scratch_shapes=[
             pltpu.VMEM((8, HALO, 384), BF),
-            pltpu.VMEM((8, HALO, OWN), BF),
-            pltpu.VMEM((8, HALO, OWN), BF),
-            pltpu.VMEM((8, HALO, OWN), BF),
+            pltpu.VMEM((8, HALO // 2, 2 * OWN), BF),
+            pltpu.VMEM((8, HALO // 2, 2 * OWN), BF),
+            pltpu.VMEM((8, HALO // 2, 2 * OWN), BF),
             pltpu.VMEM((8, 9, 4, SLOT, 2 * OWN), BF),
             pltpu.VMEM((8, 9, 4, SLOT // 2, 2 * OWN), BF),
             pltpu.VMEM((HALO, 8 * 768), BF),
-            pltpu.VMEM((2, len(PAIRS), OWN, WIN), BF),
+            pltpu.VMEM((2, len(PAIRS), 256, WIN), BF),
             pltpu.VMEM((CELLS, 2 * OWN), F32),
             pltpu.VMEM((2, CELLS, 2 * OWN), F32),
             pltpu.VMEM((CELLS, OWN), F32),

time: 206 us -> 197 us (0.956)
  Pallas kernels: 191 us -> 182 us
    pallas_call x1, Pallas kernels: 191 us -> 182 us  [local(): pl.pallas_call(kernel, out_shape=jax.ShapeDtypeStruct((2, CELLS, OWN), BF...]
where the time goes in v4:
time: 197 us; the launch traced here: 194 us
  Pallas kernels  182 us (92%)
  local copies, waits for them, and re-layouts  9.43 us (5%)
  other arithmetic  2.17 us (1%)
    pallas_call x1, Pallas kernels, local(): pl.pallas_call(kernel, out_shape=jax.ShapeDtypeStruct((2, CELLS, OWN), BF...  182 us

profile of v4, /device:TPU:31, one launch (start us, length us, event | category | flops | bytes accessed | tf_op | source)
XLA Modules:
  0.0 193.5 jit_solution(1648221584078122882)
XLA Ops:
  0.0 1.4 copy.16
  1.4 0.4 reshape.33
  1.8 0.0 copy-start
  1.8 1.0 copy.17
  2.8 0.1 fusion
  2.9 0.8 pad_maximum_fusion.wc_ref
  3.7 0.0 copy-done
  3.7 0.4 copy.14
  4.1 0.6 reshape.31
  4.7 0.0 copy-start.2
  4.7 1.2 copy.15
  6.0 0.0 copy-start.1
  6.0 0.0 copy-start.3
  6.0 0.0 copy-start.4
  6.0 0.3 reshape.32
  6.3 0.8 pad.12.wg_ref
  7.2 0.0 copy-done.2
  7.2 0.1 reshape.27
  7.3 0.1 copy.20
  7.3 0.1 reshape.28
  7.5 0.1 copy.13
  7.6 0.0 copy-done.1
  7.6 0.2 reshape.29
  7.7 0.1 copy.12
  7.9 0.1 pad.20.clone
  8.0 0.1 pad.22.clone
  8.1 0.8 maximum_maximum_fusion.act_ref
  8.8 0.0 copy-done.4
  8.8 0.6 select_maximum_fusion.bias_ref
  9.4 181.8 %shard_map.64 = bf16[2,288,192]{2,1,0:T(8,128)(2,1)} custom-call(bf16[288,384]{1,0:T(8,128)(2,1)} %maximum_maximum_fusion.act_ref, bf16[9,64,384]{2,1,0:T(8,128)(2,1)} %pad.12.wg_ref, bf16[9,32,384]{2,1,0:T(8,128)(2,1)} %pad_maximum_fusion.wc_ref, f32[8,256]{1,0:T(8,128)} %select_maximum_fusion.bias_ref), custom_call_target="tpu_custom_call" | custom-call | tf_op jit(solution)/shard_map/pallas_call | solution.py:547
  191.2 1.2 copy.18
  192.3 1.2 reshape.35
  (3 shorter events, 0.0 us)
Async XLA Ops:
  1.8 1.9 copy-start
  4.7 2.4 %copy-start.2 = (bf16[2,3,4608]{2,0,1:T(2,128)(2,1)S(1)}, bf16[2,3,4608]{2,0,1:T(2,128)(2,1)}, u32[]{:S(2)}) copy-start(bf16[2,3,4608]{2,0,1:T(2,128)(2,1)} %param.7) | copy-start | bytes 165892
  6.0 1.6 copy-start.1
  6.0 2.9 %copy-start.3 = (f32[2,192]{1,0:T(2,128)S(1)}, f32[2,192]{1,0:T(2,128)}, u32[]{:S(2)}) copy-start(f32[2,192]{1,0:T(2,128)} %param.9) | copy-start | bytes 4612
  6.0 2.8 %copy-start.4 = (f32[192]{0:T(256)S(1)}, f32[192]{0:T(256)}, u32[]{:S(2)}) copy-start(f32[192]{0:T(256)} %param.11) | copy-start | bytes 2308

commit v5 on v4

--- a/solution.py
+++ b/solution.py
@@ -449,11 +449,14 @@
             emat[order, q] = hit.astype(F32).astype(BF)
     acc[...] = jnp.zeros_like(acc)
     cacc[...] = jnp.zeros_like(cacc)
-    exchange_rest(0, init)
-    kernel_relay(1)
-    kernel_sides(0, 1)
-    kernel_own(1, True, 0)
-    kernel_own(1, True, 1)
+
+    def more_kernel():
+        kernel_sides(0, 1)
+        kernel_relay(1)
+        kernel_own(1, True, 0)
+        kernel_own(1, True, 1)
+
+    exchange_rest(0, init, more_kernel)
     sent(*first_copy)
     bias_copy.wait()
     exchanged(0, init)

time: 197 us -> 199 us (1.010)
  Pallas kernels: 182 us -> 184 us
    pallas_call x1, Pallas kernels: 182 us -> 184 us  [local(): pl.pallas_call(kernel, out_shape=jax.ShapeDtypeStruct((2, CELLS, OWN), BF...]
where the time goes in v5:
time: 199 us; the launch traced here: 196 us
  Pallas kernels  184 us (92%)
  local copies, waits for them, and re-layouts  9.43 us (5%)
  other arithmetic  2.17 us (1%)
    pallas_call x1, Pallas kernels, local(): pl.pallas_call(kernel, out_shape=jax.ShapeDtypeStruct((2, CELLS, OWN), BF...  184 us

profile of v5, /device:TPU:31, one launch (start us, length us, event | category | flops | bytes accessed | tf_op | source)
XLA Modules:
  0.0 195.5 jit_solution(10646092315237181897)
XLA Ops:
  0.0 1.4 copy.16
  1.4 0.4 reshape.33
  1.8 0.0 copy-start
  1.8 1.0 copy.17
  2.8 0.1 fusion
  2.9 0.8 pad_maximum_fusion.wc_ref
  3.7 0.0 copy-done
  3.7 0.4 copy.14
  4.1 0.6 reshape.31
  4.7 0.0 copy-start.2
  4.7 1.2 copy.15
  6.0 0.0 copy-start.1
  6.0 0.0 copy-start.3
  6.0 0.0 copy-start.4
  6.0 0.3 reshape.32
  6.3 0.8 pad.12.wg_ref
  7.2 0.0 copy-done.2
  7.2 0.1 reshape.27
  7.3 0.1 copy.20
  7.3 0.1 reshape.28
  7.5 0.1 copy.13
  7.6 0.0 copy-done.1
  7.6 0.2 reshape.29
  7.7 0.1 copy.12
  7.9 0.1 pad.20.clone
  8.0 0.1 pad.22.clone
  8.1 0.8 maximum_maximum_fusion.act_ref
  8.8 0.0 copy-done.3
  8.8 0.6 select_maximum_fusion.bias_ref
  9.4 183.8 %shard_map.64 = bf16[2,288,192]{2,1,0:T(8,128)(2,1)} custom-call(bf16[288,384]{1,0:T(8,128)(2,1)} %maximum_maximum_fusion.act_ref, bf16[9,64,384]{2,1,0:T(8,128)(2,1)} %pad.12.wg_ref, bf16[9,32,384]{2,1,0:T(8,128)(2,1)} %pad_maximum_fusion.wc_ref, f32[8,256]{1,0:T(8,128)} %select_maximum_fusion.bias_ref), custom_call_target="tpu_custom_call" | custom-call | tf_op jit(solution)/shard_map/pallas_call | solution.py:550
  193.2 1.2 copy.18
  194.3 1.2 reshape.35
  (3 shorter events, 0.0 us)
Async XLA Ops:
  1.8 1.9 copy-start
  4.7 2.4 %copy-start.2 = (bf16[2,3,4608]{2,0,1:T(2,128)(2,1)S(1)}, bf16[2,3,4608]{2,0,1:T(2,128)(2,1)}, u32[]{:S(2)}) copy-start(bf16[2,3,4608]{2,0,1:T(2,128)(2,1)} %param.7) | copy-start | bytes 165892
  6.0 1.6 copy-start.1
  6.0 2.9 %copy-start.3 = (f32[2,192]{1,0:T(2,128)S(1)}, f32[2,192]{1,0:T(2,128)}, u32[]{:S(2)}) copy-start(f32[2,192]{1,0:T(2,128)} %param.9) | copy-start | bytes 4612
  6.0 2.8 %copy-start.4 = (f32[192]{0:T(256)S(1)}, f32[192]{0:T(256)}, u32[]{:S(2)}) copy-start(f32[192]{0:T(256)} %param.11) | copy-start | bytes 2308
